TPU v7x, 768 devices: a whole 4x8x12 slice. The times are simulated.
768 devices in a mesh: rows: 12 (over z), cols: 64 (over x, y, core).
Axes of the slice: x: 4, y: 8, z: 12, core: 2. Of those that a mesh axis runs over, the one named last changes fastest.
Arguments:
- tile_values: bfloat16 [12, 64, 4, 128, 128], P('rows', 'cols'), may hold values from 0.0009994507 to 0.019897461
- tile_rows: int32 [12, 64, 4], P('rows', 'cols'), may hold values from 0 to 7, as said below
- tile_cols: int32 [12, 64, 4], P('rows', 'cols'), may hold values from 0 to 3, as said below
- live_counts: int32 [12, 64], P('rows', 'cols'), may hold values from 1 to 4, as said below
- test_block: float32 [32768, 512], P('cols'), may hold values from -6 to 6
Outputs:
- y_sample: float32 [12288, 512], P(('rows', 'cols'))
- z_power: float32 [32768, 512], P('cols')
- panel_gram: float32 [12, 512, 512], P('rows')
Inputs may be any that keep to these rules, and one draw needn't show every extreme that they name: Within one device the pairs (tile_rows, tile_cols) of its slots are distinct. `tile_cols`: column block of a slot within the device's columns. `live_counts`: some device uses all 4 slots.
All inputs are finite; a program needn't handle non-finite values.
Results may differ from a plain program's by a relative error of at most 0.0003.
Values sent between devices are 32-bit elements; how exact they have to be, the bound alone decides.
No kernel may reach another device: no remote copies, remote signals or barrier semaphores. Data moves between devices by JAX's collectives and lax.ppermute only.
A program may use at most 32 MiB of HBM per device.

v0:
```python
import jax
import jax.numpy as jnp
from jax import lax
from jax.sharding import PartitionSpec as P

RB_DEV = 8
CB_DEV = 4


def local(tile_values, tile_rows, tile_cols, live_counts, test_block):
    high = lax.Precision.HIGHEST
    tile_data = tile_values[0, 0]
    rows_local = tile_rows[0, 0]
    cols_local = tile_cols[0, 0]
    live_count = live_counts[0, 0]
    slots_here = tile_data.shape[0]
    test_cols = test_block.shape[1]
    keep_mask = (jnp.arange(slots_here, dtype=jnp.int32) < live_count).astype(jnp.float32)
    tiles_f = tile_data.astype(jnp.float32)
    picked = test_block.reshape(CB_DEV, 128, test_cols)[cols_local]
    products = jnp.einsum("sab,sbk->sak", tiles_f, picked, precision=high)
    row_onehot = (rows_local[:, None] == jnp.arange(RB_DEV, dtype=jnp.int32)[None, :]).astype(
        jnp.float32
    ) * keep_mask[:, None]
    partial_value = jnp.einsum("sr,sak->rak", row_onehot, products, precision=high).reshape(
        RB_DEV * 128, test_cols
    )
    y_shard = lax.psum_scatter(partial_value, "cols", scatter_dimension=0, tiled=True)
    local_gram = jnp.dot(y_shard.T, y_shard, precision=high, preferred_element_type=jnp.float32)
    gram = lax.psum(local_gram, "cols") / (RB_DEV * 128)
    y_panel = lax.all_gather(y_shard, "cols", axis=0, tiled=True)
    y_tiles = y_panel.reshape(RB_DEV, 128, test_cols)[rows_local]
    z_terms = jnp.einsum("sab,sak->sbk", tiles_f, y_tiles, precision=high)
    col_onehot = (cols_local[:, None] == jnp.arange(CB_DEV, dtype=jnp.int32)[None, :]).astype(
        jnp.float32
    ) * keep_mask[:, None]
    z_local = jnp.einsum("sc,sbk->cbk", col_onehot, z_terms, precision=high).reshape(
        CB_DEV * 128, test_cols
    )
    z_power = lax.psum(z_local, "rows")
    return (y_shard, z_power, gram[None])


def solution(mesh):
    return jax.shard_map(
        local,
        mesh=mesh,
        in_specs=(
            P("rows", "cols", None, None, None),
            P("rows", "cols", None),
            P("rows", "cols", None),
            P("rows", "cols"),
            P("cols", None),
        ),
        out_specs=(P(("rows", "cols"), None), P("cols", None), P("rows", None, None)),
        check_vma=False,
    )
```

profile of v0, /device:TPU:2, one launch (start us, length us, event | category | flops | bytes accessed | tf_op | source)
XLA Modules:
  0.0 606.2 jit_solution(3687051408444583402)
XLA Ops:
  7.2 0.0 copy-start
  7.2 0.0 copy-start.1
  7.2 0.0 reduce-scatter.2.cloned.1.call-start
  8.0 0.7 fusion.18
  8.7 0.6 gather_fusion
  9.3 0.0 copy-start.2
  9.3 1.0 fusion.6
  10.3 0.5 copy.10
  10.8 0.0 copy-done.2
  10.8 2.3 fusion.2
  13.2 2.6 copy.8
  15.7 0.0 reduce-scatter.2.cloned.1.call-update
  15.7 0.0 all-gather.2.cloned.1.call-start
  15.8 162.7 %reduce-scatter.2.cloned.1.call-done = f32[16,512]{1,0:T(8,128)} async-done(((f32[1024,512]{1,0:T(8,128)}), f32[16,512]{1,0:T(8,128)}) %reduce-scatter.2.cloned.1.call-update) | async-done | bytes 32784 | tf_op jit(solution)/shard_map/reduce_scatter | solution.py:28
  178.5 0.0 all-gather.2.cloned.1.call-update
  178.5 0.0 all-reduce.5.cloned.1.call-start
  178.6 2.8 fusion.22
  181.4 0.0 all-reduce.5.cloned.1.call-update
  181.5 0.0 all-reduce.3.cloned.1.call-start
  181.5 89.0 %all-gather.2.cloned.1.call-done = f32[1024,512]{1,0:T(8,128)} async-done(((f32[16,512]{1,0:T(8,128)}), f32[1024,512]{1,0:T(8,128)}) %all-gather.2.cloned.1.call-update) | async-done | bytes 2097168 | tf_op jit(solution)/shard_map/all_gather | solution.py:31
  270.5 2.2 gather_fusion.1
  272.7 0.0 copy-start.3
  272.7 1.0 fusion.4
  273.7 0.5 copy.11
  274.2 0.0 copy-done.3
  274.2 1.8 fusion
  276.0 1.3 copy.9
  277.3 0.0 all-reduce.3.cloned.1.call-update
  277.3 203.9 %all-reduce.5.cloned.1.call-done = f32[512,512]{1,0:T(8,128)} async-done(((f32[512,512]{1,0:T(8,128)}), f32[512,512]{1,0:T(8,128)}) %all-reduce.5.cloned.1.call-update) | async-done | bytes 1048592 | tf_op jit(solution)/shard_map/psum | solution.py:30
  481.2 2.3 multiply_bitcast_fusion
  483.5 113.9 %all-reduce.3.cloned.1.call-done = f32[512,512]{1,0:T(8,128)} async-done(((f32[512,512]{1,0:T(8,128)}), f32[512,512]{1,0:T(8,128)}) %all-reduce.3.cloned.1.call-update) | async-done | bytes 1048592 | tf_op jit(solution)/shard_map/psum | solution.py:40
  597.4 2.3 copy.15
  (6 shorter events, 0.0 us)
Async XLA Ops:
  7.2 1.5 copy-start
  7.2 2.1 copy-start.1
  7.2 171.3 %reduce-scatter.2.cloned.1.call-start = ((), (), s32[]{:S(2)}) async-start(), calls=%async_computation.1 | async-start | bytes 2129920 | tf_op jit(solution)/shard_map/reduce_scatter | solution.py:28
  9.3 1.5 copy-start.2
  15.7 254.7 %all-gather.2.cloned.1.call-start = ((), (), s32[]{:S(2)}) async-start(), calls=%async_computation.2 | async-start | bytes 2129920 | tf_op jit(solution)/shard_map/all_gather | solution.py:31
  178.5 302.7 %all-reduce.5.cloned.1.call-start = ((), (), s32[]{:S(2)}) async-start(), calls=%async_computation.4 | async-start | bytes 2097152 | tf_op jit(solution)/shard_map/psum | solution.py:30
  181.5 415.9 %all-reduce.3.cloned.1.call-start = ((), (), s32[]{:S(2)}) async-start(), calls=%async_computation.3 | async-start | bytes 2097152 | tf_op jit(solution)/shard_map/psum | solution.py:40
  272.7 1.5 copy-start.3
Sparse Core Ops, SparseCore 0:
  15.9 162.6 reduce-scatter.1
  183.7 86.7 all-gather.1
  274.9 206.2 all-reduce.4
  484.0 113.3 all-reduce.2
where the time goes:
time: 606 us
  waiting for transfers between devices  570 us (94%)
  between operations  14.6 us (2%)
  local copies, waits for them, and re-layouts  9.95 us (2%)
  matrix products  8.97 us (1%)
    psum x1, waiting for transfers between devices, local(): gram = lax.psum(local_gram, 'cols') / (RB_DEV * 128)  204 us
    reduce_scatter x1, waiting for transfers between devices, local(): lax.psum_scatter(partial_value, 'cols', scatter_dimension=0, tiled=True)  163 us
    psum x1, waiting for transfers between devices, local(): z_power = lax.psum(z_local, 'rows')  114 us
    all_gather x1, waiting for transfers between devices, local(): y_panel = lax.all_gather(y_shard, 'cols', axis=0, tiled=True)  89 us
  transfers between devices with their start and end apart: 4, of which 4 were waited for; matrix products, arithmetic and copies ran while one was open for 2% of the time, Pallas kernels for 0%

commit v1 on v0

v1 whole, which is shorter than its diff:
```python
import jax
import jax.numpy as jnp
from jax import lax
from jax.experimental import pallas as pl
from jax.experimental.pallas import tpu as pltpu
from jax.sharding import Mesh, PartitionSpec as P

RB_DEV = 8
CB_DEV = 4
BLK = 128
PIECES = 64


def split3(v):
    hi = v.astype(jnp.bfloat16)
    rest = v - hi.astype(jnp.float32)
    mid = rest.astype(jnp.bfloat16)
    lo = (rest - mid.astype(jnp.float32)).astype(jnp.bfloat16)
    return hi, mid, lo


def dot3(tile, v, dims):
    hi, mid, lo = split3(v)
    acc = lax.dot_general(tile, lo, dims, preferred_element_type=jnp.float32)
    acc += lax.dot_general(tile, mid, dims, preferred_element_type=jnp.float32)
    return acc + lax.dot_general(tile, hi, dims, preferred_element_type=jnp.float32)


def sample_kernel(rows_ref, cols_ref, live_ref, core_ref, tile_ref, omega_ref, keep_ref, send_ref):
    own = core_ref[0] == 0
    width = omega_ref.shape[1]
    sub = keep_ref.shape[0] // RB_DEV
    part = sub // 4
    keep_ref[...] = jnp.zeros_like(keep_ref)
    send_ref[...] = jnp.zeros_like(send_ref)
    for s in range(tile_ref.shape[0]):

        @pl.when(s < live_ref[0])
        def _():
            base = pl.multiple_of(cols_ref[s] * BLK, BLK)
            prod = dot3(tile_ref[s], omega_ref[pl.ds(base, BLK), :], (((1,), (0,)), ((), ())))
            halves = prod.reshape(4, 2, part, width)
            first = halves[:, 0].reshape(sub, width)
            second = halves[:, 1].reshape(sub, width)
            at = pl.ds(pl.multiple_of(rows_ref[s] * sub, sub), sub)
            keep_ref[at, :] += jnp.where(own, first, second)
            send_ref[at, :] += jnp.where(own, second, first)


def power_kernel(rows_ref, cols_ref, live_ref, core_ref, tile_ref, own_ref, other_ref, *refs):
    out_refs, acc_ref = refs[:-1], refs[-1]
    own = core_ref[0] == 0
    width = own_ref.shape[1]
    sub = own_ref.shape[0] // RB_DEV
    part = sub // 4
    acc_ref[...] = jnp.zeros_like(acc_ref)
    for s in range(tile_ref.shape[0]):

        @pl.when(s < live_ref[0])
        def _():
            at = pl.ds(pl.multiple_of(rows_ref[s] * sub, sub), sub)
            mine, theirs = own_ref[at, :], other_ref[at, :]
            first = jnp.where(own, mine, theirs).reshape(4, part, width)
            second = jnp.where(own, theirs, mine).reshape(4, part, width)
            y_block = jnp.stack([first, second], axis=1).reshape(BLK, width)
            term = dot3(tile_ref[s], y_block, (((0,), (0,)), ((), ())))
            base = pl.multiple_of(cols_ref[s] * BLK, BLK)
            acc_ref[pl.ds(base, BLK), :] += term

    at = 0
    for ref in out_refs:
        ref[...] = acc_ref[at : at + ref.shape[0], :]
        at += ref.shape[0]


def join_kernel(*refs):
    out_ref = refs[-1]
    at = 0
    for ref in refs[:-1]:
        out_ref[at : at + ref.shape[0], :] = ref[...]
        at += ref.shape[0]


VMEM = pl.BlockSpec(memory_space=pltpu.VMEM)
SMEM = pl.BlockSpec(memory_space=pltpu.SMEM)


def make_local(nx, ny, nc):
    def local(tile_values, tile_rows, tile_cols, live_counts, test_block):
        f32 = jnp.float32
        width = test_block.shape[1]
        panel = RB_DEV * BLK
        share = panel // (nx * ny * nc)
        half = panel // nc
        tiles = tile_values[0, 0]
        core = lax.axis_index("core").astype(jnp.int32)[None]
        scalars = (tile_rows[0, 0], tile_cols[0, 0], live_counts[0], core)
        swap = [(0, 1), (1, 0)]

        half_shape = jax.ShapeDtypeStruct((half, width), f32)
        keep, send = pl.pallas_call(
            sample_kernel,
            out_shape=(half_shape, half_shape),
            in_specs=[SMEM] * 4 + [VMEM] * 2,
            out_specs=(VMEM, VMEM),
            name="sample",
        )(*scalars, tiles, test_block)
        part = keep + lax.ppermute(send, "core", swap)
        part = lax.all_to_all(part.reshape(nx, half // nx, width), "x", 0, 0, tiled=True).sum(0)
        part = lax.all_to_all(part.reshape(ny, share, width), "y", 0, 0, tiled=True)
        y_shard = part.sum(0)

        own = jnp.broadcast_to(y_shard[None], (ny, share, width))
        own = lax.all_to_all(own, "y", 0, 0, tiled=True).reshape(ny * share, width)
        own = jnp.broadcast_to(own[None], (nx, ny * share, width))
        own = lax.all_to_all(own, "x", 0, 0, tiled=True).reshape(half, width)
        other = lax.ppermute(own, "core", swap)

        high = lax.Precision.HIGH
        gram = jnp.dot(own.T, own, precision=high, preferred_element_type=f32)
        gram = (gram + jnp.dot(other.T, other, precision=high, preferred_element_type=f32)) / panel

        rows_out = CB_DEV * BLK
        step = rows_out // PIECES
        sizes = [step] * (PIECES - 1) + [step // 2] * 2
        pieces = pl.pallas_call(
            power_kernel,
            out_shape=tuple(jax.ShapeDtypeStruct((n, width), f32) for n in sizes),
            in_specs=[SMEM] * 4 + [VMEM] * 3,
            out_specs=tuple(VMEM for _ in sizes),
            scratch_shapes=[pltpu.VMEM((rows_out, width), f32)],
            name="power",
        )(*scalars, tiles, own, other)
        pieces = lax.psum(pieces, "z")
        z_power = pl.pallas_call(
            join_kernel,
            out_shape=jax.ShapeDtypeStruct((rows_out, width), f32),
            in_specs=[VMEM] * len(sizes),
            out_specs=VMEM,
            name="join",
        )(*pieces)
        return (y_shard, z_power, gram[None])

    return local


def solution(mesh):
    rows, cols = mesh.shape["rows"], mesh.shape["cols"]
    ny, nc = 8, 2
    nx = cols // (ny * nc)
    grid = Mesh(mesh.devices.reshape(rows, nx, ny, nc), ("z", "x", "y", "core"))
    split = ("x", "y", "core")
    return jax.shard_map(
        make_local(nx, ny, nc),
        mesh=grid,
        in_specs=(
            P("z", split, None, None, None),
            P("z", split, None),
            P("z", split, None),
            P("z", split),
            P(split, None),
        ),
        out_specs=(P(("z",) + split, None), P(split, None), P("z", None, None)),
        check_vma=False,
    )
```

time: 606 us -> 155 us (0.26)
  the two profiles are of different devices: /device:TPU:2 before, /device:TPU:8 now
where the time goes in v1:
time: 155 us; the launch traced here: 154 us
  blocking collectives  128 us (83%)
  Pallas kernels  9.43 us (6%)
  waiting for transfers between devices  4.41 us (3%)
  starting transfers between devices  3.82 us (2%)
  matrix products  3.04 us (2%)
  local copies, waits for them, and re-layouts  2.46 us (2%)
    psum x1, blocking collectives, local(): pieces = lax.psum(pieces, 'z')  60 us
    all_to_all x1, blocking collectives, local(): part = lax.all_to_all(part.reshape(ny, share, width), 'y', 0, 0, tiled=True)  20.9 us
    all_to_all x1, blocking collectives, local(): lax.all_to_all(part.reshape(nx, half // nx, width), 'x', 0, 0, tiled=True)  19.2 us
    all_to_all x1, blocking collectives, local(): own = lax.all_to_all(own, 'x', 0, 0, tiled=True).reshape(half, width)  14.9 us
    all_to_all x1, blocking collectives, local(): own = lax.all_to_all(own, 'y', 0, 0, tiled=True).reshape(ny * share, width)  12.9 us
    pallas_call x1, Pallas kernels, local(): pl.pallas_call(sample_kernel, out_shape=(half_shape, half_shape), in_spec...  3.61 us
    pallas_call x1, Pallas kernels, local(): pl.pallas_call(power_kernel, out_shape=tuple((jax.ShapeDtypeStruct((n, wi...  3.51 us
  transfers between devices with their start and end apart: 2, of which 2 were waited for; matrix products, arithmetic and copies ran while one was open for 1% of the time, Pallas kernels for 0%

profile of v1, /device:TPU:8, one launch (start us, length us, event | category | flops | bytes accessed | tf_op | source)
XLA Modules:
  0.0 154.1 jit_solution(6601249713507405382)
XLA Ops:
  1.3 3.6 %sample.1 = (f32[512,512]{1,0:T(8,128)}, f32[512,512]{1,0:T(8,128)}) custom-call(s32[4]{0:T(128)} %bitcast.26, s32[4]{0:T(128)} %bitcast.28, s32[1]{0:T(128)} %bitcast.17.live_ref, s32[1]{0:T(128)} %bitcast.3.core_ref, bf16[4,128,128]{2,1,0:T(8,128)(2,1)} %bitcast.24, f32[512,512]{1,0:T(8,128)} %omega_ref.1), custom_call_target="tpu_custom_call" | custom-call | tf_op jit(solution)/shard_map/sample/pallas_call | solution.py:101
  4.9 1.9 %collective-permute-start = (f32[512,512]{1,0:T(8,128)}, f32[512,512]{1,0:T(8,128)S(1)}, u32[]{:S(2)}, u32[]{:S(2)}) collective-permute-start(f32[512,512]{1,0:T(8,128)} %get-tuple-element.71), channel_id=1, source_target_pairs={{0,1},{1,0},{2,3},{3,2},{4,5},{5,4},{6,7},{7,6},{8,9},{9,8},{10,11... | collective-permute-start | bytes 3145736 | tf_op jit(solution)/shard_map/ppermute | solution.py:108
  6.8 2.8 %collective-permute-done = f32[512,512]{1,0:T(8,128)S(1)} collective-permute-done((f32[512,512]{1,0:T(8,128)}, f32[512,512]{1,0:T(8,128)S(1)}, u32[]{:S(2)}, u32[]{:S(2)}) %collective-permute-start) | collective-permute-done | bytes 1048608 | tf_op jit(solution)/shard_map/ppermute | solution.py:108
  9.6 1.4 add.136
  11.1 19.2 %all_to_all.20 = f32[4,128,512]{2,1,0:T(8,128)S(1)} all-to-all(f32[4,128,512]{2,1,0:T(8,128)S(1)} %bitcast.21), channel_id=1, replica_groups=mesh['z'=12,'x'=4,'y'=8,'core'=2] {'x'}, dimensions={0} | all-to-all | bytes 2097152 | tf_op jit(solution)/shard_map/all_to_all | solution.py:109
  30.3 0.1 reduce_sum.18
  30.4 20.9 %all_to_all.21 = f32[8,16,512]{2,1,0:T(8,128)S(1)} all-to-all(f32[8,16,512]{2,1,0:T(8,128)S(1)} %bitcast.22), channel_id=1, replica_groups=mesh['z'=12,'x'=4,'y'=8,'core'=2] {'y'}, dimensions={0} | all-to-all | bytes 524288 | tf_op jit(solution)/shard_map/all_to_all | solution.py:110
  51.3 0.0 copy-start.3
  51.4 0.6 copy-done.3
  52.0 12.9 %all_to_all.22 = f32[8,16,512]{2,1,0:T(8,128)S(1)} all-to-all(f32[8,16,512]{2,1,0:T(8,128)S(1)} %broadcast_in_dim.20), channel_id=1, replica_groups=mesh['z'=12,'x'=4,'y'=8,'core'=2] {'y'}, dimensions={0} | all-to-all | bytes 524288 | tf_op jit(solution)/shard_map/all_to_all | solution.py:114
  64.8 0.1 broadcast_in_dim.22
  65.0 14.9 %all_to_all.23 = f32[4,128,512]{2,1,0:T(8,128)S(1)} all-to-all(f32[4,128,512]{2,1,0:T(8,128)S(1)} %broadcast_in_dim.22), channel_id=1, replica_groups=mesh['z'=12,'x'=4,'y'=8,'core'=2] {'x'}, dimensions={0} | all-to-all | bytes 2097152 | tf_op jit(solution)/shard_map/all_to_all | solution.py:116
  79.8 1.9 %collective-permute-start.1 = (f32[512,512]{1,0:T(8,128)S(1)}, f32[512,512]{1,0:T(8,128)S(1)}, u32[]{:S(2)}, u32[]{:S(2)}) collective-permute-start(f32[512,512]{1,0:T(8,128)S(1)} %bitcast.19), channel_id=1, source_target_pairs={{0,1},{1,0},{2,3},{3,2},{4,5},{5,4},{6,7},{7,6},{8,9},{9,8},{10,11... | collective-permute-start | bytes 3145736 | tf_op jit(solution)/shard_map/ppermute | solution.py:117
  81.8 1.0 convolution_bitcast_fusion
  82.8 0.0 copy-done
  82.8 1.6 %collective-permute-done.1.other_ref = f32[512,512]{1,0:T(8,128)S(1)} collective-permute-done((f32[512,512]{1,0:T(8,128)S(1)}, f32[512,512]{1,0:T(8,128)S(1)}, u32[]{:S(2)}, u32[]{:S(2)}) %collective-permute-start.1) | collective-permute-done | bytes 1048608 | tf_op jit(solution)/shard_map/ppermute | solution.py:117
  84.4 1.0 copy-done.1
  85.4 3.5 %power.1 = (f32[8,512]{1,0:T(8,128)}, f32[8,512]{1,0:T(8,128)}, f32[8,512]{1,0:T(8,128)}, f32[8,512]{1,0:T(8,128)}, f32[8,512]{1,0:T(8,128)}, /*index=5*/f32[8,5...) custom-call(s32[4]{0:T(128)} %bitcast.27, ...), custom_call_target="tpu_custom_call" | custom-call | tf_op jit(solution)/shard_map/power/pallas_call | solution.py:126
  88.9 0.0 copy-start.4
  88.9 0.0 copy-start.5
  88.9 0.6 copy-done.11
  89.6 0.0 copy-done.10
  89.6 0.0 copy-done.9
  89.6 0.0 copy-done.8
  89.6 0.0 copy-done.7
  89.6 0.0 copy-done.6
  89.7 0.0 copy-done.4
  89.7 0.0 copy-done.5
  89.7 60.0 %all-reduce.2 = (f32[8,512]{1,0:T(8,128)}, f32[8,512]{1,0:T(8,128)}, f32[8,512]{1,0:T(8,128)}, f32[8,512]{1,0:T(8,128)}, f32[8,512]{1,0:T(8,128)}, /*index=5*/f3...) all-reduce(f32[8,512]{1,0:T(8,128)S(1)} %copy-done.4, ...), channel_id=1, replica_groups=mesh['z'=12,'x'=4,'y'=8,'core'=2] {'z'}, use_global_device_ids=true, to_apply=%region_2.0 | all-reduce | flops 262144 | bytes 2097152 | tf_op jit(solution)/shard_map/psum | solution.py:134
  149.7 2.3 %join.1 = f32[512,512]{1,0:T(8,128)} custom-call(f32[8,512]{1,0:T(8,128)} %get-tuple-element.137.refs_0_, f32[8,512]{1,0:T(8,128)} %get-tuple-element.138.refs_1_, f32[8,512]{1,0:T(8,128)} %get-tuple-element.139.refs_2_, f32[8,512]{1,0:T(8,128)} %get-tuple-element.140.refs_3_, f32[8,512]{1,0:T(8,128)} %get-tuple-element.141.refs_4_, ...), custom_call_target="tpu_custom_call" | custom-call | tf_op jit(solution)/shard_map/join/pallas_call | solution.py:135
  152.1 0.0 copy-done.2
  152.1 2.0 %fusion.1 = f32[1,512,512]{2,1,0:T(8,128)} fusion(f32[512,512]{1,0:T(8,128)S(1)} %convolution_bitcast_fusion, f32[512,512]{1,0:T(8,128)S(1)} %copy-done.2), kind=kOutput, calls=%fused_computation.2 | convolution fusion | flops 805830656 | bytes 3145728 | tf_op jit(solution)/shard_map/dot_general | solution.py:121
  (11 shorter events, 0.1 us)
Async XLA Ops:
  4.9 4.8 %collective-permute-start = (f32[512,512]{1,0:T(8,128)}, f32[512,512]{1,0:T(8,128)S(1)}, u32[]{:S(2)}, u32[]{:S(2)}) collective-permute-start(f32[512,512]{1,0:T(8,128)} %get-tuple-element.71), channel_id=1, source_target_pairs={{0,1},{1,0},{2,3},{3,2},{4,5},{5,4},{6,7},{7,6},{8,9},{9,8},{10,11... | collective-permute-start | bytes 3145736 | tf_op jit(solution)/shard_map/ppermute | solution.py:108
  51.3 0.6 copy-start.3
  79.8 3.0 %copy-start = (f32[4,128,512]{2,1,0:T(8,128)}, f32[4,128,512]{2,1,0:T(8,128)S(1)}, u32[]{:S(2)}) copy-start(f32[4,128,512]{2,1,0:T(8,128)S(1)} %all_to_all.23) | copy-start | bytes 3145732
  79.8 4.5 %collective-permute-start.1 = (f32[512,512]{1,0:T(8,128)S(1)}, f32[512,512]{1,0:T(8,128)S(1)}, u32[]{:S(2)}, u32[]{:S(2)}) collective-permute-start(f32[512,512]{1,0:T(8,128)S(1)} %bitcast.19), channel_id=1, source_target_pairs={{0,1},{1,0},{2,3},{3,2},{4,5},{5,4},{6,7},{7,6},{8,9},{9,8},{10,11... | collective-permute-start | bytes 3145736 | tf_op jit(solution)/shard_map/ppermute | solution.py:117
  84.4 1.0 copy-start.1
  88.9 0.7 copy-start.11
  88.9 0.7 copy-start.10
  88.9 0.7 copy-start.9
  88.9 0.7 copy-start.8
  88.9 0.7 copy-start.7
  88.9 0.8 copy-start.6
  88.9 0.8 copy-start.4
  88.9 0.8 copy-start.5
  149.7 2.3 %copy-start.2 = (f32[512,512]{1,0:T(8,128)S(1)}, f32[512,512]{1,0:T(8,128)}, u32[]{:S(2)}) copy-start(f32[512,512]{1,0:T(8,128)} %copy-done.1) | copy-start | bytes 3145732

commit v2 on v1

--- a/solution.py
+++ b/solution.py
@@ -50,16 +50,19 @@
 def power_kernel(rows_ref, cols_ref, live_ref, core_ref, tile_ref, own_ref, other_ref, *refs):
     out_refs, acc_ref = refs[:-1], refs[-1]
     own = core_ref[0] == 0
-    width = own_ref.shape[1]
-    sub = own_ref.shape[0] // RB_DEV
+    width = other_ref.shape[1]
+    sub = other_ref.shape[0] // RB_DEV
     part = sub // 4
+    per = own_ref.shape[1] // sub
     acc_ref[...] = jnp.zeros_like(acc_ref)
     for s in range(tile_ref.shape[0]):
 
         @pl.when(s < live_ref[0])
         def _():
             at = pl.ds(pl.multiple_of(rows_ref[s] * sub, sub), sub)
-            mine, theirs = own_ref[at, :], other_ref[at, :]
+            row = rows_ref[s]
+            mine = own_ref[row // per, pl.ds(pl.multiple_of(row % per * sub, sub), sub), :]
+            theirs = other_ref[at, :]
             first = jnp.where(own, mine, theirs).reshape(4, part, width)
             second = jnp.where(own, theirs, mine).reshape(4, part, width)
             y_block = jnp.stack([first, second], axis=1).reshape(BLK, width)
@@ -73,16 +76,30 @@
         at += ref.shape[0]
 
 
-def join_kernel(*refs):
-    out_ref = refs[-1]
-    at = 0
-    for ref in refs[:-1]:
-        out_ref[at : at + ref.shape[0], :] = ref[...]
+def finish_kernel(gram_ref, other_ref, *refs):
+    pieces, (z_ref, out_ref, sems) = refs[:-3], refs[-3:]
+    copies, at = [], 0
+    for i, ref in enumerate(pieces):
+        copies.append(pltpu.make_async_copy(ref, z_ref.at[at : at + ref.shape[0]], sems.at[i]))
         at += ref.shape[0]
+    for copy in copies:
+        copy.start()
+    v = other_ref[...]
+    hi = v.astype(jnp.bfloat16)
+    mid = (v - hi.astype(jnp.float32)).astype(jnp.bfloat16)
+    dims = (((0,), (0,)), ((), ()))
+    acc = lax.dot_general(hi, mid, dims, preferred_element_type=jnp.float32)
+    acc += lax.dot_general(mid, hi, dims, preferred_element_type=jnp.float32)
+    acc += lax.dot_general(hi, hi, dims, preferred_element_type=jnp.float32)
+    out_ref[...] = (gram_ref[...] + acc) * (1.0 / (RB_DEV * BLK))
+    for copy in copies:
+        copy.wait()
 
 
 VMEM = pl.BlockSpec(memory_space=pltpu.VMEM)
 SMEM = pl.BlockSpec(memory_space=pltpu.SMEM)
+ANY = pl.BlockSpec(memory_space=pl.ANY)
+PARAMS = pltpu.CompilerParams(vmem_limit_bytes=16 << 20)
 
 
 def make_local(nx, ny, nc):
@@ -97,7 +114,7 @@
         scalars = (tile_rows[0, 0], tile_cols[0, 0], live_counts[0], core)
         swap = [(0, 1), (1, 0)]
 
-        half_shape = jax.ShapeDtypeStruct((half, width), f32)
+        half_shape = pltpu.VMEM((half, width), f32)
         keep, send = pl.pallas_call(
             sample_kernel,
             out_shape=(half_shape, half_shape),
@@ -113,32 +130,38 @@
         own = jnp.broadcast_to(y_shard[None], (ny, share, width))
         own = lax.all_to_all(own, "y", 0, 0, tiled=True).reshape(ny * share, width)
         own = jnp.broadcast_to(own[None], (nx, ny * share, width))
-        own = lax.all_to_all(own, "x", 0, 0, tiled=True).reshape(half, width)
+        spread = lax.all_to_all(own, "x", 0, 0, tiled=True)
+        own = spread.reshape(half, width)
         other = lax.ppermute(own, "core", swap)
 
         high = lax.Precision.HIGH
         gram = jnp.dot(own.T, own, precision=high, preferred_element_type=f32)
-        gram = (gram + jnp.dot(other.T, other, precision=high, preferred_element_type=f32)) / panel
 
         rows_out = CB_DEV * BLK
         step = rows_out // PIECES
         sizes = [step] * (PIECES - 1) + [step // 2] * 2
         pieces = pl.pallas_call(
             power_kernel,
-            out_shape=tuple(jax.ShapeDtypeStruct((n, width), f32) for n in sizes),
+            out_shape=tuple(pltpu.HBM((n, width), f32) for n in sizes),
             in_specs=[SMEM] * 4 + [VMEM] * 3,
             out_specs=tuple(VMEM for _ in sizes),
             scratch_shapes=[pltpu.VMEM((rows_out, width), f32)],
+            compiler_params=PARAMS,
             name="power",
-        )(*scalars, tiles, own, other)
+        )(*scalars, tiles, spread, other)
         pieces = lax.psum(pieces, "z")
-        z_power = pl.pallas_call(
-            join_kernel,
-            out_shape=jax.ShapeDtypeStruct((rows_out, width), f32),
-            in_specs=[VMEM] * len(sizes),
-            out_specs=VMEM,
-            name="join",
-        )(*pieces)
+        z_power, gram = pl.pallas_call(
+            finish_kernel,
+            out_shape=(
+                jax.ShapeDtypeStruct((rows_out, width), f32),
+                jax.ShapeDtypeStruct((width, width), f32),
+            ),
+            in_specs=[VMEM] * (2 + len(sizes)),
+            out_specs=(ANY, VMEM),
+            scratch_shapes=[pltpu.SemaphoreType.DMA((len(sizes),))],
+            compiler_params=PARAMS,
+            name="finish",
+        )(gram, other, *[v for v in pieces])
         return (y_shard, z_power, gram[None])
 
     return local

time: 155 us -> 148 us (0.955)
  the two profiles are of different devices: /device:TPU:8 before, /device:TPU:2 now
where the time goes in v2:
time: 148 us
  blocking collectives  128 us (86%)
  Pallas kernels  7.7 us (5%)
  waiting for transfers between devices  4.07 us (3%)
  starting transfers between devices  4.04 us (3%)
  local copies, waits for them, and re-layouts  1.5 us (1%)
    psum x1, blocking collectives, local(): pieces = lax.psum(pieces, 'z')  59.3 us
    all_to_all x1, blocking collectives, local(): lax.all_to_all(part.reshape(nx, half // nx, width), 'x', 0, 0, tiled=True)  26.4 us
    all_to_all x1, blocking collectives, local(): spread = lax.all_to_all(own, 'x', 0, 0, tiled=True)  15 us
    all_to_all x1, blocking collectives, local(): part = lax.all_to_all(part.reshape(ny, share, width), 'y', 0, 0, tiled=True)  14 us
    all_to_all x1, blocking collectives, local(): own = lax.all_to_all(own, 'y', 0, 0, tiled=True).reshape(ny * share, width)  12.9 us
  transfers between devices with their start and end apart: 2, of which 2 were waited for; matrix products, arithmetic and copies ran while one was open for 1% of the time, Pallas kernels for 0%

profile of v2, /device:TPU:2, one launch (start us, length us, event | category | flops | bytes accessed | tf_op | source)
XLA Modules:
  0.0 147.8 jit_solution(12615742293314068120)
XLA Ops:
  1.3 2.3 %sample.1 = (f32[512,512]{1,0:T(8,128)S(1)}, f32[512,512]{1,0:T(8,128)S(1)}) custom-call(s32[4]{0:T(128)} %bitcast.19, s32[4]{0:T(128)} %bitcast.21, s32[1]{0:T(128)} %bitcast.14.live_ref, s32[1]{0:T(128)} %bitcast.3.core_ref, bf16[4,128,128]{2,1,0:T(8,128)(2,1)} %bitcast.17, f32[512,512]{1,0:T(8,128)} %omega_ref.1), custom_call_target="tpu_custom_call" | custom-call | tf_op jit(solution)/shard_map/sample/pallas_call | solution.py:118
  3.6 2.0 %collective-permute-start = (f32[512,512]{1,0:T(8,128)S(1)}, f32[512,512]{1,0:T(8,128)S(1)}, u32[]{:S(2)}, u32[]{:S(2)}) collective-permute-start(f32[512,512]{1,0:T(8,128)S(1)} %get-tuple-element.73), channel_id=1, source_target_pairs={{0,1},{1,0},{2,3},{3,2},{4,5},{5,4},{6,7},{7,6},{8,9},{9,8},{10,11... | collective-permute-start | bytes 3145736 | tf_op jit(solution)/shard_map/ppermute | solution.py:125
  5.6 2.5 %collective-permute-done = f32[512,512]{1,0:T(8,128)S(1)} collective-permute-done((f32[512,512]{1,0:T(8,128)S(1)}, f32[512,512]{1,0:T(8,128)S(1)}, u32[]{:S(2)}, u32[]{:S(2)}) %collective-permute-start) | collective-permute-done | bytes 1048608 | tf_op jit(solution)/shard_map/ppermute | solution.py:125
  8.1 0.2 add.133
  8.4 26.4 %all_to_all.20 = f32[4,128,512]{2,1,0:T(8,128)S(1)} all-to-all(f32[4,128,512]{2,1,0:T(8,128)S(1)} %bitcast.23), channel_id=1, replica_groups=mesh['z'=12,'x'=4,'y'=8,'core'=2] {'x'}, dimensions={0} | all-to-all | bytes 2097152 | tf_op jit(solution)/shard_map/all_to_all | solution.py:126
  34.8 0.1 reduce_sum.18
  34.9 14.0 %all_to_all.21 = f32[8,16,512]{2,1,0:T(8,128)S(1)} all-to-all(f32[8,16,512]{2,1,0:T(8,128)S(1)} %bitcast.24), channel_id=1, replica_groups=mesh['z'=12,'x'=4,'y'=8,'core'=2] {'y'}, dimensions={0} | all-to-all | bytes 524288 | tf_op jit(solution)/shard_map/all_to_all | solution.py:127
  48.9 0.0 copy-start.3
  49.0 0.6 copy-done.3
  49.6 12.9 %all_to_all.22 = f32[8,16,512]{2,1,0:T(8,128)S(1)} all-to-all(f32[8,16,512]{2,1,0:T(8,128)S(1)} %broadcast_in_dim.20), channel_id=1, replica_groups=mesh['z'=12,'x'=4,'y'=8,'core'=2] {'y'}, dimensions={0} | all-to-all | bytes 524288 | tf_op jit(solution)/shard_map/all_to_all | solution.py:131
  62.4 0.1 broadcast_in_dim.22
  62.6 15.0 %all_to_all.23.own_ref = f32[4,128,512]{2,1,0:T(8,128)S(1)} all-to-all(f32[4,128,512]{2,1,0:T(8,128)S(1)} %broadcast_in_dim.22), channel_id=1, replica_groups=mesh['z'=12,'x'=4,'y'=8,'core'=2] {'x'}, dimensions={0} | all-to-all | bytes 2097152 | tf_op jit(solution)/shard_map/all_to_all | solution.py:133
  77.6 2.0 %collective-permute-start.1 = (f32[512,512]{1,0:T(8,128)S(1)}, f32[512,512]{1,0:T(8,128)S(1)}, u32[]{:S(2)}, u32[]{:S(2)}) collective-permute-start(f32[512,512]{1,0:T(8,128)S(1)} %bitcast.16), channel_id=1, source_target_pairs={{0,1},{1,0},{2,3},{3,2},{4,5},{5,4},{6,7},{7,6},{8,9},{9,8},{10,11... | collective-permute-start | bytes 3145736 | tf_op jit(solution)/shard_map/ppermute | solution.py:135
  79.6 1.1 convolution_bitcast_fusion.gram_ref
  80.7 0.0 copy-start.1
  80.7 0.0 copy-start.2
  80.7 1.5 %collective-permute-done.1.other_ref = f32[512,512]{1,0:T(8,128)S(1)} collective-permute-done((f32[512,512]{1,0:T(8,128)S(1)}, f32[512,512]{1,0:T(8,128)S(1)}, u32[]{:S(2)}, u32[]{:S(2)}) %collective-permute-start.1) | collective-permute-done | bytes 1048608 | tf_op jit(solution)/shard_map/ppermute | solution.py:135
  82.2 0.0 copy-done
  82.2 0.0 copy-done.1
  82.2 2.6 %power.1 = (f32[8,512]{1,0:T(8,128)}, f32[8,512]{1,0:T(8,128)}, f32[8,512]{1,0:T(8,128)}, f32[8,512]{1,0:T(8,128)}, f32[8,512]{1,0:T(8,128)}, /*index=5*/f32[8,5...) custom-call(s32[4]{0:T(128)S(1)} %bitcast.20, ...), custom_call_target="tpu_custom_call" | custom-call | tf_op jit(solution)/shard_map/power/pallas_call | solution.py:143
  84.9 0.0 copy-start.4
  84.9 0.0 copy-start.5
  84.9 0.6 copy-done.11
  85.5 0.0 copy-done.10
  85.6 0.0 copy-done.9
  85.6 0.0 copy-done.8
  85.6 0.0 copy-done.7
  85.6 0.0 copy-done.6
  85.6 0.0 copy-done.4
  85.7 0.0 copy-done.5
  85.7 59.3 %all-reduce.2 = (f32[8,512]{1,0:T(8,128)S(1)}, f32[8,512]{1,0:T(8,128)S(1)}, f32[8,512]{1,0:T(8,128)S(1)}, f32[8,512]{1,0:T(8,128)S(1)}, f32[8,512]{1,0:T(8,128)...) all-reduce(f32[8,512]{1,0:T(8,128)S(1)} %copy-done.4, ...), channel_id=1, replica_groups=mesh['z'=12,'x'=4,'y'=8,'core'=2] {'z'}, use_global_device_ids=true, to_apply=%region_2.0 | all-reduce | flops 262144 | bytes 2097152 | tf_op jit(solution)/shard_map/psum | solution.py:152
  145.0 2.8 %finish.1 = (f32[512,512]{1,0:T(8,128)}, f32[512,512]{1,0:T(8,128)}) custom-call(f32[512,512]{1,0:T(8,128)S(1)} %convolution_bitcast_fusion.gram_ref, f32[512,512]{1,0:T(8,128)S(1)} %collective-permute-done.1.other_ref, f32[8,512]{1,0:T(8,128)S(1)} %get-tuple-element.141.refs_0_, f32[8,512]{1,0:T(8,128)S(1)} %get-tuple-element.142.refs_1_, ...), custom_call_target="tpu_custom_call" | custom-call | tf_op jit(solution)/shard_map/finish/pallas_call | solution.py:153
  (10 shorter events, 0.1 us)
Async XLA Ops:
  3.6 4.6 %collective-permute-start = (f32[512,512]{1,0:T(8,128)S(1)}, f32[512,512]{1,0:T(8,128)S(1)}, u32[]{:S(2)}, u32[]{:S(2)}) collective-permute-start(f32[512,512]{1,0:T(8,128)S(1)} %get-tuple-element.73), channel_id=1, source_target_pairs={{0,1},{1,0},{2,3},{3,2},{4,5},{5,4},{6,7},{7,6},{8,9},{9,8},{10,11... | collective-permute-start | bytes 3145736 | tf_op jit(solution)/shard_map/ppermute | solution.py:125
  48.9 0.6 copy-start.3
  77.6 4.7 %copy-start = (bf16[1,1,4,128,128]{4,3,2,1,0:T(8,128)(2,1)S(1)}, bf16[1,1,4,128,128]{4,3,2,1,0:T(8,128)(2,1)}, u32[]{:S(2)}) copy-start(bf16[1,1,4,128,128]{4,3,2,1,0:T(8,128)(2,1)} %param.5) | copy-start | bytes 393220
  77.6 4.7 %collective-permute-start.1 = (f32[512,512]{1,0:T(8,128)S(1)}, f32[512,512]{1,0:T(8,128)S(1)}, u32[]{:S(2)}, u32[]{:S(2)}) collective-permute-start(f32[512,512]{1,0:T(8,128)S(1)} %bitcast.16), channel_id=1, source_target_pairs={{0,1},{1,0},{2,3},{3,2},{4,5},{5,4},{6,7},{7,6},{8,9},{9,8},{10,11... | collective-permute-start | bytes 3145736 | tf_op jit(solution)/shard_map/ppermute | solution.py:135
  80.7 1.6 %copy-start.1 = (s32[1,1,4]{2,1,0:T(1,128)S(1)}, s32[1,1,4]{2,1,0:T(1,128)}, u32[]{:S(2)}) copy-start(s32[1,1,4]{2,1,0:T(1,128)} %param.6) | copy-start | bytes 52
  80.7 1.5 %copy-start.2 = (s32[1,1,4]{2,1,0:T(1,128)S(1)}, s32[1,1,4]{2,1,0:T(1,128)}, u32[]{:S(2)}) copy-start(s32[1,1,4]{2,1,0:T(1,128)} %param.7) | copy-start | bytes 52
  84.8 0.7 copy-start.11
  84.8 0.7 copy-start.10
  84.9 0.7 copy-start.9
  84.9 0.7 copy-start.8
  84.9 0.7 copy-start.7
  84.9 0.8 copy-start.6
  84.9 0.8 copy-start.4
  84.9 0.8 copy-start.5

commit v3 on v1

v3 whole, which is shorter than its diff:
```python
import jax
import jax.numpy as jnp
from jax import lax
from jax.experimental import pallas as pl
from jax.experimental.pallas import tpu as pltpu
from jax.sharding import Mesh, PartitionSpec as P

RB_DEV = 8
CB_DEV = 4
BLK = 128
PIECES = 64


def tile_dot(tile, v, axis):
    hi = v.astype(jnp.bfloat16)
    mid = (v - hi.astype(jnp.float32)).astype(jnp.bfloat16)
    dims = (((axis,), (0,)), ((), ()))
    return lax.dot_general(
        jnp.concatenate([tile, tile], axis=axis),
        jnp.concatenate([hi, mid], axis=0),
        dims,
        preferred_element_type=jnp.float32,
    )


def sample_kernel(rows_ref, cols_ref, live_ref, core_ref, tile_ref, omega_ref, keep_ref, send_ref):
    own = core_ref[0] == 0
    width = omega_ref.shape[1]
    sub = keep_ref.shape[0] // RB_DEV
    part = sub // 4
    keep_ref[...] = jnp.zeros_like(keep_ref)
    send_ref[...] = jnp.zeros_like(send_ref)
    for s in range(tile_ref.shape[0]):

        @pl.when(s < live_ref[0])
        def _():
            base = pl.multiple_of(cols_ref[s] * BLK, BLK)
            halves = tile_dot(tile_ref[s], omega_ref[pl.ds(base, BLK), :], 1).reshape(4, 2, part, width)
            first = halves[:, 0].reshape(sub, width)
            second = halves[:, 1].reshape(sub, width)
            at = pl.ds(pl.multiple_of(rows_ref[s] * sub, sub), sub)
            keep_ref[at, :] += jnp.where(own, first, second)
            send_ref[at, :] += jnp.where(own, second, first)


def power_kernel(
    rows_ref, cols_ref, live_ref, core_ref, tile_ref, own_ref, other_ref, gram_ref, y_ref, *refs
):
    out_refs, (gram_out, y_out, acc_ref, gram_buf, sems) = refs[:-5], refs[-5:]
    y_copy = pltpu.make_async_copy(y_ref, y_out, sems.at[0])
    y_copy.start()
    chunks, per, sub, width = other_ref.shape
    part = sub // 4
    v = other_ref[...].reshape(per * chunks * sub, width)
    hi = v.astype(jnp.bfloat16)
    mid = (v - hi.astype(jnp.float32)).astype(jnp.bfloat16)
    dims = (((0,), (0,)), ((), ()))
    acc = lax.dot_general(hi, mid, dims, preferred_element_type=jnp.float32)
    acc += lax.dot_general(mid, hi, dims, preferred_element_type=jnp.float32)
    acc += lax.dot_general(hi, hi, dims, preferred_element_type=jnp.float32)
    gram_buf[...] = (gram_ref[...] + acc) * (1.0 / (RB_DEV * BLK))
    gram_copy = pltpu.make_async_copy(gram_buf, gram_out, sems.at[1])
    gram_copy.start()

    own = core_ref[0] == 0
    acc_ref[...] = jnp.zeros_like(acc_ref)
    for s in range(tile_ref.shape[0]):

        @pl.when(s < live_ref[0])
        def _():
            row = rows_ref[s]
            mine, theirs = own_ref[row // per, row % per], other_ref[row // per, row % per]
            first = jnp.where(own, mine, theirs).reshape(4, part, width)
            second = jnp.where(own, theirs, mine).reshape(4, part, width)
            y_block = jnp.stack([first, second], axis=1).reshape(BLK, width)
            base = pl.multiple_of(cols_ref[s] * BLK, BLK)
            acc_ref[pl.ds(base, BLK), :] += tile_dot(tile_ref[s], y_block, 0)

    at = 0
    for ref in out_refs:
        ref[...] = acc_ref[at : at + ref.shape[0], :]
        at += ref.shape[0]
    y_copy.wait()
    gram_copy.wait()


def join_kernel(*refs):
    pieces, (z_ref, sems) = refs[:-2], refs[-2:]
    copies, at = [], 0
    for i, ref in enumerate(pieces):
        copies.append(pltpu.make_async_copy(ref, z_ref.at[at : at + ref.shape[0]], sems.at[i]))
        at += ref.shape[0]
    for copy in copies:
        copy.start()
    for copy in copies:
        copy.wait()


VMEM = pl.BlockSpec(memory_space=pltpu.VMEM)
SMEM = pl.BlockSpec(memory_space=pltpu.SMEM)
ANY = pl.BlockSpec(memory_space=pl.ANY)
PARAMS = pltpu.CompilerParams(vmem_limit_bytes=16 << 20)


def make_local(nx, ny, nc):
    def local(tile_values, tile_rows, tile_cols, live_counts, test_block):
        f32 = jnp.float32
        width = test_block.shape[1]
        panel = RB_DEV * BLK
        share = panel // (nx * ny * nc)
        half = panel // nc
        tiles = tile_values[0, 0]
        core = lax.axis_index("core").astype(jnp.int32)[None]
        scalars = (tile_rows[0, 0], tile_cols[0, 0], live_counts[0], core)
        swap = [(0, 1), (1, 0)]

        half_shape = pltpu.VMEM((half, width), f32)
        keep, send = pl.pallas_call(
            sample_kernel,
            out_shape=(half_shape, half_shape),
            in_specs=[SMEM] * 4 + [VMEM] * 2,
            out_specs=(VMEM, VMEM),
            name="sample",
        )(*scalars, tiles, test_block)
        part = keep + lax.ppermute(send, "core", swap)
        part = lax.all_to_all(part.reshape(nx, half // nx, width), "x", 0, 0, tiled=True).sum(0)
        part = lax.all_to_all(part.reshape(ny, share, width), "y", 0, 0, tiled=True)
        y_shard = part.sum(0)

        own = jnp.broadcast_to(y_shard[None], (ny, share, width))
        own = lax.all_to_all(own, "y", 0, 0, tiled=True)
        sub = half // RB_DEV
        own = own.reshape(RB_DEV // nx, 1, sub, width)
        own = jnp.broadcast_to(own.reshape(1, -1, width), (nx, half // nx, width))
        own = lax.all_to_all(own, "x", 0, 0, tiled=True).reshape(nx, RB_DEV // nx, sub, width)
        other = lax.ppermute(own, "core", swap)

        flat = own.reshape(half, width)
        gram = jnp.dot(flat.T, flat, precision=lax.Precision.HIGH, preferred_element_type=f32)

        rows_out = CB_DEV * BLK
        step = rows_out // PIECES
        sizes = [step] * (PIECES - 1) + [step // 2] * 2
        *pieces, gram, y_out = pl.pallas_call(
            power_kernel,
            out_shape=tuple(jax.ShapeDtypeStruct((n, width), f32) for n in sizes)
            + (
                jax.ShapeDtypeStruct((width, width), f32),
                jax.ShapeDtypeStruct((share, width), f32),
            ),
            in_specs=[SMEM] * 4 + [VMEM] * 5,
            out_specs=tuple(VMEM for _ in sizes) + (ANY, ANY),
            scratch_shapes=[
                pltpu.VMEM((rows_out, width), f32),
                pltpu.VMEM((width, width), f32),
                pltpu.SemaphoreType.DMA((2,)),
            ],
            compiler_params=PARAMS,
            name="power",
        )(*scalars, tiles, own, other, gram, y_shard)
        pieces = lax.psum(pieces, "z")
        z_power = pl.pallas_call(
            join_kernel,
            out_shape=jax.ShapeDtypeStruct((rows_out, width), f32),
            in_specs=[VMEM] * len(sizes),
            out_specs=ANY,
            scratch_shapes=[pltpu.SemaphoreType.DMA((len(sizes),))],
            compiler_params=PARAMS,
            name="join",
        )(*pieces)
        return (y_out, z_power, gram[None])

    return local


def solution(mesh):
    rows, cols = mesh.shape["rows"], mesh.shape["cols"]
    ny, nc = 8, 2
    nx = cols // (ny * nc)
    grid = Mesh(mesh.devices.reshape(rows, nx, ny, nc), ("z", "x", "y", "core"))
    split = ("x", "y", "core")
    return jax.shard_map(
        make_local(nx, ny, nc),
        mesh=grid,
        in_specs=(
            P("z", split, None, None, None),
            P("z", split, None),
            P("z", split, None),
            P("z", split),
            P(split, None),
        ),
        out_specs=(P(("z",) + split, None), P(split, None), P("z", None, None)),
        check_vma=False,
    )
```

time: 155 us -> 146 us (0.942)
  the two profiles are of different devices: /device:TPU:8 before, /device:TPU:2 now
where the time goes in v3:
time: 146 us; the launch traced here: 145 us
  blocking collectives  128 us (88%)
  Pallas kernels  6.33 us (4%)
  waiting for transfers between devices  4.15 us (3%)
  starting transfers between devices  3.96 us (3%)
    psum x1, blocking collectives, local(): pieces = lax.psum(pieces, 'z')  59.9 us
    all_to_all x1, blocking collectives, local(): lax.all_to_all(part.reshape(nx, half // nx, width), 'x', 0, 0, tiled=True)  26.2 us
    all_to_all x1, blocking collectives, local(): lax.all_to_all(own, 'x', 0, 0, tiled=True)  15 us
    all_to_all x1, blocking collectives, local(): part = lax.all_to_all(part.reshape(ny, share, width), 'y', 0, 0, tiled=True)  14 us
    all_to_all x1, blocking collectives, local(): own = lax.all_to_all(own, 'y', 0, 0, tiled=True)  12.9 us
  transfers between devices with their start and end apart: 2, of which 2 were waited for; matrix products, arithmetic and copies ran while one was open for 1% of the time, Pallas kernels for 0%

profile of v3, /device:TPU:2, one launch (start us, length us, event | category | flops | bytes accessed | tf_op | source)
XLA Modules:
  0.0 145.3 jit_solution(13201589349497883521)
XLA Ops:
  1.3 2.1 %sample.1 = (f32[512,512]{1,0:T(8,128)S(1)}, f32[512,512]{1,0:T(8,128)S(1)}) custom-call(s32[4]{0:T(128)} %bitcast.20, s32[4]{0:T(128)} %bitcast.22, s32[1]{0:T(128)} %bitcast.14.live_ref, s32[1]{0:T(128)} %bitcast.3.core_ref, bf16[4,128,128]{2,1,0:T(8,128)(2,1)} %bitcast.18, f32[512,512]{1,0:T(8,128)} %omega_ref.1), custom_call_target="tpu_custom_call" | custom-call | tf_op jit(solution)/shard_map/sample/pallas_call | solution.py:118
  3.3 1.9 %collective-permute-start = (f32[512,512]{1,0:T(8,128)S(1)}, f32[512,512]{1,0:T(8,128)S(1)}, u32[]{:S(2)}, u32[]{:S(2)}) collective-permute-start(f32[512,512]{1,0:T(8,128)S(1)} %get-tuple-element.73), channel_id=1, source_target_pairs={{0,1},{1,0},{2,3},{3,2},{4,5},{5,4},{6,7},{7,6},{8,9},{9,8},{10,11... | collective-permute-start | bytes 3145736 | tf_op jit(solution)/shard_map/ppermute | solution.py:125
  5.3 2.6 %collective-permute-done = f32[512,512]{1,0:T(8,128)S(1)} collective-permute-done((f32[512,512]{1,0:T(8,128)S(1)}, f32[512,512]{1,0:T(8,128)S(1)}, u32[]{:S(2)}, u32[]{:S(2)}) %collective-permute-start) | collective-permute-done | bytes 1048608 | tf_op jit(solution)/shard_map/ppermute | solution.py:125
  7.9 0.2 add.133
  8.1 26.2 %all_to_all.20 = f32[4,128,512]{2,1,0:T(8,128)S(1)} all-to-all(f32[4,128,512]{2,1,0:T(8,128)S(1)} %bitcast.24), channel_id=1, replica_groups=mesh['z'=12,'x'=4,'y'=8,'core'=2] {'x'}, dimensions={0} | all-to-all | bytes 2097152 | tf_op jit(solution)/shard_map/all_to_all | solution.py:126
  34.3 0.1 reduce_sum.18
  34.4 14.0 %all_to_all.21 = f32[8,16,512]{2,1,0:T(8,128)S(1)} all-to-all(f32[8,16,512]{2,1,0:T(8,128)S(1)} %bitcast.25), channel_id=1, replica_groups=mesh['z'=12,'x'=4,'y'=8,'core'=2] {'y'}, dimensions={0} | all-to-all | bytes 524288 | tf_op jit(solution)/shard_map/all_to_all | solution.py:127
  48.5 12.9 %all_to_all.22 = f32[8,16,512]{2,1,0:T(8,128)S(1)} all-to-all(f32[8,16,512]{2,1,0:T(8,128)S(1)} %broadcast_in_dim.20), channel_id=1, replica_groups=mesh['z'=12,'x'=4,'y'=8,'core'=2] {'y'}, dimensions={0} | all-to-all | bytes 524288 | tf_op jit(solution)/shard_map/all_to_all | solution.py:131
  61.4 0.1 broadcast_in_dim.22
  61.5 15.0 %all_to_all.23 = f32[4,128,512]{2,1,0:T(8,128)S(1)} all-to-all(f32[4,128,512]{2,1,0:T(8,128)S(1)} %broadcast_in_dim.22), channel_id=1, replica_groups=mesh['z'=12,'x'=4,'y'=8,'core'=2] {'x'}, dimensions={0} | all-to-all | bytes 2097152 | tf_op jit(solution)/shard_map/all_to_all | solution.py:135
  76.5 0.0 copy-start
  76.5 2.0 %collective-permute-start.1 = (f32[4,2,64,512]{3,2,1,0:T(8,128)S(1)}, f32[4,2,64,512]{3,2,1,0:T(8,128)S(1)}, u32[]{:S(2)}, u32[]{:S(2)}) collective-permute-start(f32[4,2,64,512]{3,2,1,0:T(8,128)S(1)} %bitcast.16), channel_id=1, source_target_pairs={{0,1},{1,0},{2,3},{3,2},{4,5},{5,4},{6,7},{7,6},{8,9},{9,8},{10,11... | collective-permute-start | bytes 3145736 | tf_op jit(solution)/shard_map/ppermute | solution.py:136
  78.5 1.1 convolution_bitcast_fusion.gram_ref
  79.6 0.0 copy-start.1
  79.6 0.0 copy-start.2
  79.6 1.5 %collective-permute-done.1.other_ref = f32[4,2,64,512]{3,2,1,0:T(8,128)S(1)} collective-permute-done((f32[4,2,64,512]{3,2,1,0:T(8,128)S(1)}, f32[4,2,64,512]{3,2,1,0:T(8,128)S(1)}, u32[]{:S(2)}, u32[]{:S(2)}) %collective-permute-start.1) | collective-permute-done | bytes 1048608 | tf_op jit(solution)/shard_map/ppermute | solution.py:136
  81.1 0.0 copy-done
  81.2 0.0 copy-done.1
  81.2 0.0 copy-done.2
  81.2 2.7 %power.1 = (f32[8,512]{1,0:T(8,128)S(1)}, f32[8,512]{1,0:T(8,128)S(1)}, f32[8,512]{1,0:T(8,128)S(1)}, f32[8,512]{1,0:T(8,128)S(1)}, f32[8,512]{1,0:T(8,128)S(1)}...) custom-call(s32[4]{0:T(128)S(1)} %bitcast.21, ...), custom_call_target="tpu_custom_call" | custom-call | tf_op jit(solution)/shard_map/power/pallas_call | solution.py:144
  83.9 59.9 %all-reduce.2 = (f32[8,512]{1,0:T(8,128)S(1)}, f32[8,512]{1,0:T(8,128)S(1)}, f32[8,512]{1,0:T(8,128)S(1)}, f32[8,512]{1,0:T(8,128)S(1)}, f32[8,512]{1,0:T(8,128)...) all-reduce(f32[8,512]{1,0:T(8,128)S(1)} %get-tuple-element.75, ...), channel_id=1, replica_groups=mesh['z'=12,'x'=4,'y'=8,'core'=2] {'z'}, use_global_device_ids=true, to_apply=%region_2.0 | all-reduce | flops 262144 | bytes 2097152 | tf_op jit(solution)/shard_map/psum | solution.py:161
  143.8 1.6 %join.1 = f32[512,512]{1,0:T(8,128)} custom-call(f32[8,512]{1,0:T(8,128)S(1)} %get-tuple-element.141.refs_0_, f32[8,512]{1,0:T(8,128)S(1)} %get-tuple-element.142.refs_1_, f32[8,512]{1,0:T(8,128)S(1)} %get-tuple-element.143.refs_2_, f32[8,512]{1,0:T(8,128)S(1)} %get-tuple-element.144.refs_3_, f32[8,512]{1,0:T(8,128)S(1)} %get-tuple-element.145.refs_4_, ...), custom_call_target="tpu_custom_call" | custom-call | tf_op jit(solution)/shard_map/join/pallas_call | solution.py:162
  (2 shorter events, 0.0 us)
Async XLA Ops:
  3.3 4.6 %collective-permute-start = (f32[512,512]{1,0:T(8,128)S(1)}, f32[512,512]{1,0:T(8,128)S(1)}, u32[]{:S(2)}, u32[]{:S(2)}) collective-permute-start(f32[512,512]{1,0:T(8,128)S(1)} %get-tuple-element.73), channel_id=1, source_target_pairs={{0,1},{1,0},{2,3},{3,2},{4,5},{5,4},{6,7},{7,6},{8,9},{9,8},{10,11... | collective-permute-start | bytes 3145736 | tf_op jit(solution)/shard_map/ppermute | solution.py:125
  76.5 4.7 %copy-start = (bf16[1,1,4,128,128]{4,3,2,1,0:T(8,128)(2,1)S(1)}, bf16[1,1,4,128,128]{4,3,2,1,0:T(8,128)(2,1)}, u32[]{:S(2)}) copy-start(bf16[1,1,4,128,128]{4,3,2,1,0:T(8,128)(2,1)} %param.5) | copy-start | bytes 393220
  76.5 4.7 %collective-permute-start.1 = (f32[4,2,64,512]{3,2,1,0:T(8,128)S(1)}, f32[4,2,64,512]{3,2,1,0:T(8,128)S(1)}, u32[]{:S(2)}, u32[]{:S(2)}) collective-permute-start(f32[4,2,64,512]{3,2,1,0:T(8,128)S(1)} %bitcast.16), channel_id=1, source_target_pairs={{0,1},{1,0},{2,3},{3,2},{4,5},{5,4},{6,7},{7,6},{8,9},{9,8},{10,11... | collective-permute-start | bytes 3145736 | tf_op jit(solution)/shard_map/ppermute | solution.py:136
  79.6 1.6 %copy-start.1 = (s32[1,1,4]{2,1,0:T(1,128)S(1)}, s32[1,1,4]{2,1,0:T(1,128)}, u32[]{:S(2)}) copy-start(s32[1,1,4]{2,1,0:T(1,128)} %param.6) | copy-start | bytes 52
  79.6 1.5 %copy-start.2 = (s32[1,1,4]{2,1,0:T(1,128)S(1)}, s32[1,1,4]{2,1,0:T(1,128)}, u32[]{:S(2)}) copy-start(s32[1,1,4]{2,1,0:T(1,128)} %param.7) | copy-start | bytes 52

commit v4 on v3

--- a/solution.py
+++ b/solution.py
@@ -35,12 +35,15 @@
         @pl.when(s < live_ref[0])
         def _():
             base = pl.multiple_of(cols_ref[s] * BLK, BLK)
-            halves = tile_dot(tile_ref[s], omega_ref[pl.ds(base, BLK), :], 1).reshape(4, 2, part, width)
-            first = halves[:, 0].reshape(sub, width)
-            second = halves[:, 1].reshape(sub, width)
-            at = pl.ds(pl.multiple_of(rows_ref[s] * sub, sub), sub)
-            keep_ref[at, :] += jnp.where(own, first, second)
-            send_ref[at, :] += jnp.where(own, second, first)
+            halves = tile_dot(tile_ref[s], omega_ref[pl.ds(base, BLK), :], 1).reshape(2, 2, 2, part, width)
+            row = rows_ref[s]
+            for odd in range(2):
+                first = halves[:, odd, 0].reshape(2 * part, width)
+                second = halves[:, odd, 1].reshape(2 * part, width)
+                at = (row // 2 * 2 + odd) * sub + row % 2 * (2 * part)
+                at = pl.ds(pl.multiple_of(at, 2 * part), 2 * part)
+                keep_ref[at, :] += jnp.where(own, first, second)
+                send_ref[at, :] += jnp.where(own, second, first)
 
 
 def power_kernel(
@@ -49,9 +52,9 @@
     out_refs, (gram_out, y_out, acc_ref, gram_buf, sems) = refs[:-5], refs[-5:]
     y_copy = pltpu.make_async_copy(y_ref, y_out, sems.at[0])
     y_copy.start()
-    chunks, per, sub, width = other_ref.shape
+    places, sub, width = other_ref.shape
     part = sub // 4
-    v = other_ref[...].reshape(per * chunks * sub, width)
+    v = other_ref[...].reshape(places * sub, width)
     hi = v.astype(jnp.bfloat16)
     mid = (v - hi.astype(jnp.float32)).astype(jnp.bfloat16)
     dims = (((0,), (0,)), ((), ()))
@@ -69,10 +72,13 @@
         @pl.when(s < live_ref[0])
         def _():
             row = rows_ref[s]
-            mine, theirs = own_ref[row // per, row % per], other_ref[row // per, row % per]
-            first = jnp.where(own, mine, theirs).reshape(4, part, width)
-            second = jnp.where(own, theirs, mine).reshape(4, part, width)
-            y_block = jnp.stack([first, second], axis=1).reshape(BLK, width)
+            at = pl.ds(pl.multiple_of(row % 2 * (2 * part), 2 * part), 2 * part)
+            parts = []
+            for odd in range(2):
+                mine, theirs = own_ref[row // 2 * 2 + odd, at, :], other_ref[row // 2 * 2 + odd, at, :]
+                parts.append(jnp.where(own, mine, theirs).reshape(2, part, width))
+                parts.append(jnp.where(own, theirs, mine).reshape(2, part, width))
+            y_block = jnp.stack(parts, axis=1).reshape(BLK, width)
             base = pl.multiple_of(cols_ref[s] * BLK, BLK)
             acc_ref[pl.ds(base, BLK), :] += tile_dot(tile_ref[s], y_block, 0)
 
@@ -123,16 +129,16 @@
             name="sample",
         )(*scalars, tiles, test_block)
         part = keep + lax.ppermute(send, "core", swap)
-        part = lax.all_to_all(part.reshape(nx, half // nx, width), "x", 0, 0, tiled=True).sum(0)
-        part = lax.all_to_all(part.reshape(ny, share, width), "y", 0, 0, tiled=True)
+        near, far = nx * 2, ny // 2
+        part = part.reshape(near, half // near, width)
+        part = lax.all_to_all(part, ("x", "odd"), 0, 0, tiled=True).sum(0)
+        part = lax.all_to_all(part.reshape(far, share, width), "pair", 0, 0, tiled=True)
         y_shard = part.sum(0)
 
-        own = jnp.broadcast_to(y_shard[None], (ny, share, width))
-        own = lax.all_to_all(own, "y", 0, 0, tiled=True)
-        sub = half // RB_DEV
-        own = own.reshape(RB_DEV // nx, 1, sub, width)
-        own = jnp.broadcast_to(own.reshape(1, -1, width), (nx, half // nx, width))
-        own = lax.all_to_all(own, "x", 0, 0, tiled=True).reshape(nx, RB_DEV // nx, sub, width)
+        own = jnp.broadcast_to(y_shard[None], (far, share, width))
+        own = lax.all_to_all(own, "pair", 0, 0, tiled=True).reshape(1, far * share, width)
+        own = jnp.broadcast_to(own, (near, far * share, width))
+        own = lax.all_to_all(own, ("x", "odd"), 0, 0, tiled=True)
         other = lax.ppermute(own, "core", swap)
 
         flat = own.reshape(half, width)
@@ -177,8 +183,8 @@
     rows, cols = mesh.shape["rows"], mesh.shape["cols"]
     ny, nc = 8, 2
     nx = cols // (ny * nc)
-    grid = Mesh(mesh.devices.reshape(rows, nx, ny, nc), ("z", "x", "y", "core"))
-    split = ("x", "y", "core")
+    grid = Mesh(mesh.devices.reshape(rows, nx, ny // 2, 2, nc), ("z", "x", "pair", "odd", "core"))
+    split = ("x", "pair", "odd", "core")
     return jax.shard_map(
         make_local(nx, ny, nc),
         mesh=grid,

time: 146 us -> 143 us (0.979)
  the two profiles are of different devices: /device:TPU:2 before, /device:TPU:8 now
where the time goes in v4:
time: 143 us
  blocking collectives  126 us (88%)
  Pallas kernels  5.95 us (4%)
  starting transfers between devices  4.38 us (3%)
  waiting for transfers between devices  3.79 us (3%)
    psum x1, blocking collectives, local(): pieces = lax.psum(pieces, 'z')  61.3 us
    all_to_all x1, blocking collectives, local(): part = lax.all_to_all(part, ('x', 'odd'), 0, 0, tiled=True).sum(0)  27.3 us
    all_to_all x1, blocking collectives, local(): own = lax.all_to_all(own, ('x', 'odd'), 0, 0, tiled=True)  15 us
    all_to_all x1, blocking collectives, local(): lax.all_to_all(part.reshape(far, share, width), 'pair', 0, 0, tiled=True)  11.3 us
    all_to_all x1, blocking collectives, local(): lax.all_to_all(own, 'pair', 0, 0, tiled=True).reshape(1, far * share, width)  10.9 us
  transfers between devices with their start and end apart: 2, of which 2 were waited for; matrix products, arithmetic and copies ran while one was open for 1% of the time, Pallas kernels for 0%

profile of v4, /device:TPU:8, one launch (start us, length us, event | category | flops | bytes accessed | tf_op | source)
XLA Modules:
  0.0 142.9 jit_solution(4242004780504191396)
XLA Ops:
  1.3 1.7 %sample.1 = (f32[512,512]{1,0:T(8,128)S(1)}, f32[512,512]{1,0:T(8,128)S(1)}) custom-call(s32[4]{0:T(128)} %bitcast.17, s32[4]{0:T(128)} %bitcast.19, s32[1]{0:T(128)} %bitcast.13.live_ref, s32[1]{0:T(128)} %bitcast.3.core_ref, bf16[4,128,128]{2,1,0:T(8,128)(2,1)} %bitcast.15, f32[512,512]{1,0:T(8,128)} %omega_ref.1), custom_call_target="tpu_custom_call" | custom-call | tf_op jit(solution)/shard_map/sample/pallas_call | solution.py:124
  3.0 2.3 %collective-permute-start = (f32[512,512]{1,0:T(8,128)S(1)}, f32[512,512]{1,0:T(8,128)S(1)}, u32[]{:S(2)}, u32[]{:S(2)}) collective-permute-start(f32[512,512]{1,0:T(8,128)S(1)} %get-tuple-element.73), channel_id=1, source_target_pairs={{0,1},{1,0},{2,3},{3,2},{4,5},{5,4},{6,7},{7,6},{8,9},{9,8},{10,11... | collective-permute-start | bytes 3145736 | tf_op jit(solution)/shard_map/ppermute | solution.py:131
  5.3 2.3 %collective-permute-done = f32[512,512]{1,0:T(8,128)S(1)} collective-permute-done((f32[512,512]{1,0:T(8,128)S(1)}, f32[512,512]{1,0:T(8,128)S(1)}, u32[]{:S(2)}, u32[]{:S(2)}) %collective-permute-start) | collective-permute-done | bytes 1048608 | tf_op jit(solution)/shard_map/ppermute | solution.py:131
  7.6 0.2 add.133
  7.8 27.3 %all_to_all.20 = f32[8,64,512]{2,1,0:T(8,128)S(1)} all-to-all(f32[8,64,512]{2,1,0:T(8,128)S(1)} %bitcast.21), channel_id=1, replica_groups=mesh['z'=12,'x'=4,'pair'=4,'odd'=2,'core'=2] {'x','odd'}, dimensions={0} | all-to-all | bytes 2097152 | tf_op jit(solution)/shard_map/all_to_all | solution.py:134
  35.1 0.1 reduce_sum.18
  35.2 11.3 %all_to_all.21 = f32[4,16,512]{2,1,0:T(8,128)S(1)} all-to-all(f32[4,16,512]{2,1,0:T(8,128)S(1)} %bitcast.22), channel_id=1, replica_groups=mesh['z'=12,'x'=4,'pair'=4,'odd'=2,'core'=2] {'pair'}, dimensions={0} | all-to-all | bytes 262144 | tf_op jit(solution)/shard_map/all_to_all | solution.py:135
  46.5 10.9 %all_to_all.22 = f32[4,16,512]{2,1,0:T(8,128)S(1)} all-to-all(f32[4,16,512]{2,1,0:T(8,128)S(1)} %broadcast_in_dim.20), channel_id=1, replica_groups=mesh['z'=12,'x'=4,'pair'=4,'odd'=2,'core'=2] {'pair'}, dimensions={0} | all-to-all | bytes 262144 | tf_op jit(solution)/shard_map/all_to_all | solution.py:139
  57.5 0.1 broadcast_in_dim.22
  57.6 15.0 %all_to_all.23.own_ref = f32[8,64,512]{2,1,0:T(8,128)S(1)} all-to-all(f32[8,64,512]{2,1,0:T(8,128)S(1)} %broadcast_in_dim.22), channel_id=1, replica_groups=mesh['z'=12,'x'=4,'pair'=4,'odd'=2,'core'=2] {'x','odd'}, dimensions={0} | all-to-all | bytes 2097152 | tf_op jit(solution)/shard_map/all_to_all | solution.py:141
  72.6 0.0 copy-start
  72.6 2.0 %collective-permute-start.1 = (f32[8,64,512]{2,1,0:T(8,128)S(1)}, f32[8,64,512]{2,1,0:T(8,128)S(1)}, u32[]{:S(2)}, u32[]{:S(2)}) collective-permute-start(f32[8,64,512]{2,1,0:T(8,128)S(1)} %all_to_all.23.own_ref), channel_id=1, source_target_pairs={{0,1},{1,0},{2,3},{3,2},{4,5},{5,4},{6,7},{7,6},{8,9},{9,8},{10,11... | collective-permute-start | bytes 3145736 | tf_op jit(solution)/shard_map/ppermute | solution.py:142
  74.7 1.1 convolution_bitcast_fusion.gram_ref
  75.8 0.0 copy-start.1
  75.8 0.0 copy-start.2
  75.8 1.5 %collective-permute-done.1.other_ref = f32[8,64,512]{2,1,0:T(8,128)S(1)} collective-permute-done((f32[8,64,512]{2,1,0:T(8,128)S(1)}, f32[8,64,512]{2,1,0:T(8,128)S(1)}, u32[]{:S(2)}, u32[]{:S(2)}) %collective-permute-start.1) | collective-permute-done | bytes 1048608 | tf_op jit(solution)/shard_map/ppermute | solution.py:142
  77.3 0.0 copy-done
  77.3 0.0 copy-done.1
  77.3 0.0 copy-done.2
  77.3 2.7 %power.1 = (f32[8,512]{1,0:T(8,128)S(1)}, f32[8,512]{1,0:T(8,128)S(1)}, f32[8,512]{1,0:T(8,128)S(1)}, f32[8,512]{1,0:T(8,128)S(1)}, f32[8,512]{1,0:T(8,128)S(1)}...) custom-call(s32[4]{0:T(128)S(1)} %bitcast.18, ...), custom_call_target="tpu_custom_call" | custom-call | tf_op jit(solution)/shard_map/power/pallas_call | solution.py:150
  80.0 61.3 %all-reduce.2 = (f32[8,512]{1,0:T(8,128)S(1)}, f32[8,512]{1,0:T(8,128)S(1)}, f32[8,512]{1,0:T(8,128)S(1)}, f32[8,512]{1,0:T(8,128)S(1)}, f32[8,512]{1,0:T(8,128)...) all-reduce(f32[8,512]{1,0:T(8,128)S(1)} %get-tuple-element.75, ...), channel_id=1, replica_groups=mesh['z'=12,'x'=4,'pair'=4,'odd'=2,'core'=2] {'z'}, use_global_device_ids=true, to_apply=%region_2.0 | all-reduce | flops 262144 | bytes 2097152 | tf_op jit(solution)/shard_map/psum | solution.py:167
  141.3 1.6 %join.1 = f32[512,512]{1,0:T(8,128)} custom-call(f32[8,512]{1,0:T(8,128)S(1)} %get-tuple-element.141.refs_0_, f32[8,512]{1,0:T(8,128)S(1)} %get-tuple-element.142.refs_1_, f32[8,512]{1,0:T(8,128)S(1)} %get-tuple-element.143.refs_2_, f32[8,512]{1,0:T(8,128)S(1)} %get-tuple-element.144.refs_3_, f32[8,512]{1,0:T(8,128)S(1)} %get-tuple-element.145.refs_4_, ...), custom_call_target="tpu_custom_call" | custom-call | tf_op jit(solution)/shard_map/join/pallas_call | solution.py:168
  (2 shorter events, 0.0 us)
Async XLA Ops:
  3.0 4.6 %collective-permute-start = (f32[512,512]{1,0:T(8,128)S(1)}, f32[512,512]{1,0:T(8,128)S(1)}, u32[]{:S(2)}, u32[]{:S(2)}) collective-permute-start(f32[512,512]{1,0:T(8,128)S(1)} %get-tuple-element.73), channel_id=1, source_target_pairs={{0,1},{1,0},{2,3},{3,2},{4,5},{5,4},{6,7},{7,6},{8,9},{9,8},{10,11... | collective-permute-start | bytes 3145736 | tf_op jit(solution)/shard_map/ppermute | solution.py:131
  72.6 4.7 %copy-start = (bf16[1,1,4,128,128]{4,3,2,1,0:T(8,128)(2,1)S(1)}, bf16[1,1,4,128,128]{4,3,2,1,0:T(8,128)(2,1)}, u32[]{:S(2)}) copy-start(bf16[1,1,4,128,128]{4,3,2,1,0:T(8,128)(2,1)} %param.5) | copy-start | bytes 393220
  72.6 4.7 %collective-permute-start.1 = (f32[8,64,512]{2,1,0:T(8,128)S(1)}, f32[8,64,512]{2,1,0:T(8,128)S(1)}, u32[]{:S(2)}, u32[]{:S(2)}) collective-permute-start(f32[8,64,512]{2,1,0:T(8,128)S(1)} %all_to_all.23.own_ref), channel_id=1, source_target_pairs={{0,1},{1,0},{2,3},{3,2},{4,5},{5,4},{6,7},{7,6},{8,9},{9,8},{10,11... | collective-permute-start | bytes 3145736 | tf_op jit(solution)/shard_map/ppermute | solution.py:142
  75.8 1.6 %copy-start.1 = (s32[1,1,4]{2,1,0:T(1,128)S(1)}, s32[1,1,4]{2,1,0:T(1,128)}, u32[]{:S(2)}) copy-start(s32[1,1,4]{2,1,0:T(1,128)} %param.6) | copy-start | bytes 52
  75.8 1.5 %copy-start.2 = (s32[1,1,4]{2,1,0:T(1,128)S(1)}, s32[1,1,4]{2,1,0:T(1,128)}, u32[]{:S(2)}) copy-start(s32[1,1,4]{2,1,0:T(1,128)} %param.7) | copy-start | bytes 52

commit v5 on v4

--- a/solution.py
+++ b/solution.py
@@ -47,10 +47,12 @@
 
 
 def power_kernel(
-    rows_ref, cols_ref, live_ref, core_ref, tile_ref, own_ref, other_ref, gram_ref, y_ref, *refs
+    rows_ref, cols_ref, live_ref, core_ref, tile_ref, own_ref, other_ref, gram_ref, y_ref, place_ref, *refs
 ):
     out_refs, (gram_out, y_out, acc_ref, gram_buf, sems) = refs[:-5], refs[-5:]
-    y_copy = pltpu.make_async_copy(y_ref, y_out, sems.at[0])
+    share = y_out.shape[0]
+    y_at = pl.ds(pl.multiple_of(place_ref[0] * share, share), share)
+    y_copy = pltpu.make_async_copy(y_ref.at[y_at], y_out, sems.at[0])
     y_copy.start()
     places, sub, width = other_ref.shape
     part = sub // 4
@@ -117,6 +119,7 @@
         half = panel // nc
         tiles = tile_values[0, 0]
         core = lax.axis_index("core").astype(jnp.int32)[None]
+        place = lax.axis_index("pair").astype(jnp.int32)[None]
         scalars = (tile_rows[0, 0], tile_cols[0, 0], live_counts[0], core)
         swap = [(0, 1), (1, 0)]
 
@@ -132,12 +135,8 @@
         near, far = nx * 2, ny // 2
         part = part.reshape(near, half // near, width)
         part = lax.all_to_all(part, ("x", "odd"), 0, 0, tiled=True).sum(0)
-        part = lax.all_to_all(part.reshape(far, share, width), "pair", 0, 0, tiled=True)
-        y_shard = part.sum(0)
-
-        own = jnp.broadcast_to(y_shard[None], (far, share, width))
-        own = lax.all_to_all(own, "pair", 0, 0, tiled=True).reshape(1, far * share, width)
-        own = jnp.broadcast_to(own, (near, far * share, width))
+        chunk = lax.all_gather(part, "pair", axis=0, tiled=False).sum(0)
+        own = jnp.broadcast_to(chunk[None], (near, far * share, width))
         own = lax.all_to_all(own, ("x", "odd"), 0, 0, tiled=True)
         other = lax.ppermute(own, "core", swap)
 
@@ -154,7 +153,7 @@
                 jax.ShapeDtypeStruct((width, width), f32),
                 jax.ShapeDtypeStruct((share, width), f32),
             ),
-            in_specs=[SMEM] * 4 + [VMEM] * 5,
+            in_specs=[SMEM] * 4 + [VMEM] * 5 + [SMEM],
             out_specs=tuple(VMEM for _ in sizes) + (ANY, ANY),
             scratch_shapes=[
                 pltpu.VMEM((rows_out, width), f32),
@@ -163,7 +162,7 @@
             ],
             compiler_params=PARAMS,
             name="power",
-        )(*scalars, tiles, own, other, gram, y_shard)
+        )(*scalars, tiles, own, other, gram, chunk, place)
         pieces = lax.psum(pieces, "z")
         z_power = pl.pallas_call(
             join_kernel,

time: 143 us -> 137 us (0.958)
  blocking collectives: 126 us -> 119 us
    all_to_all x2 -> x0, blocking collectives: 22.3 us -> none  [the longest x1 11.3 us: local(): lax.all_to_all(part.reshape(far, share, width), 'pair', 0, 0, tiled=True)]
    all_gather x0 -> x1, blocking collectives: none -> 16.5 us  [local(): chunk = lax.all_gather(part, 'pair', axis=0, tiled=False).sum(0)]
    psum x1, blocking collectives: 61.3 us -> 59.8 us  [local(): pieces = lax.psum(pieces, 'z')]
where the time goes in v5:
time: 137 us; the launch traced here: 136 us
  blocking collectives  119 us (87%)
  Pallas kernels  6.2 us (5%)
  waiting for transfers between devices  4.18 us (3%)
  starting transfers between devices  3.85 us (3%)
    psum x1, blocking collectives, local(): pieces = lax.psum(pieces, 'z')  59.8 us
    all_to_all x1, blocking collectives, local(): part = lax.all_to_all(part, ('x', 'odd'), 0, 0, tiled=True).sum(0)  26.6 us
    all_gather x1, blocking collectives, local(): chunk = lax.all_gather(part, 'pair', axis=0, tiled=False).sum(0)  16.5 us
    all_to_all x1, blocking collectives, local(): own = lax.all_to_all(own, ('x', 'odd'), 0, 0, tiled=True)  15.6 us
  transfers between devices with their start and end apart: 2, of which 2 were waited for; matrix products, arithmetic and copies ran while one was open for 1% of the time, Pallas kernels for 0%

profile of v5, /device:TPU:8, one launch (start us, length us, event | category | flops | bytes accessed | tf_op | source)
XLA Modules:
  0.0 136.2 jit_solution(5562796670960159986)
XLA Ops:
  1.3 2.1 %sample.1 = (f32[512,512]{1,0:T(8,128)S(1)}, f32[512,512]{1,0:T(8,128)S(1)}) custom-call(s32[4]{0:T(128)} %bitcast.17, s32[4]{0:T(128)} %bitcast.19, s32[1]{0:T(128)} %bitcast.13.live_ref, s32[1]{0:T(128)} %bitcast.3.core_ref, bf16[4,128,128]{2,1,0:T(8,128)(2,1)} %bitcast.15, f32[512,512]{1,0:T(8,128)} %omega_ref.1), custom_call_target="tpu_custom_call" | custom-call | tf_op jit(solution)/shard_map/sample/pallas_call | solution.py:127
  3.4 1.9 %collective-permute-start = (f32[512,512]{1,0:T(8,128)S(1)}, f32[512,512]{1,0:T(8,128)S(1)}, u32[]{:S(2)}, u32[]{:S(2)}) collective-permute-start(f32[512,512]{1,0:T(8,128)S(1)} %get-tuple-element.73), channel_id=1, source_target_pairs={{0,1},{1,0},{2,3},{3,2},{4,5},{5,4},{6,7},{7,6},{8,9},{9,8},{10,11... | collective-permute-start | bytes 3145736 | tf_op jit(solution)/shard_map/ppermute | solution.py:134
  5.3 2.6 %collective-permute-done = f32[512,512]{1,0:T(8,128)S(1)} collective-permute-done((f32[512,512]{1,0:T(8,128)S(1)}, f32[512,512]{1,0:T(8,128)S(1)}, u32[]{:S(2)}, u32[]{:S(2)}) %collective-permute-start) | collective-permute-done | bytes 1048608 | tf_op jit(solution)/shard_map/ppermute | solution.py:134
  7.9 0.2 add.133
  8.1 26.6 %all_to_all.10 = f32[8,64,512]{2,1,0:T(8,128)S(1)} all-to-all(f32[8,64,512]{2,1,0:T(8,128)S(1)} %bitcast.21), channel_id=1, replica_groups=mesh['z'=12,'x'=4,'pair'=4,'odd'=2,'core'=2] {'x','odd'}, dimensions={0} | all-to-all | bytes 2097152 | tf_op jit(solution)/shard_map/all_to_all | solution.py:137
  34.7 0.1 reduce_sum.18
  34.8 16.5 %all-gather = f32[256,512]{1,0:T(8,128)S(1)} all-gather(f32[64,512]{1,0:T(8,128)S(1)} %reduce_sum.18), channel_id=2, replica_groups=mesh['z'=12,'x'=4,'pair'=4,'odd'=2,'core'=2] {'pair'}, dimensions={0}, use_global_device_ids=true | all-gather | bytes 655360 | tf_op jit(solution)/shard_map/all_gather | solution.py:138
  51.4 0.1 broadcast_in_dim.16
  51.5 15.6 %all_to_all.11.own_ref = f32[8,64,512]{2,1,0:T(8,128)S(1)} all-to-all(f32[8,64,512]{2,1,0:T(8,128)S(1)} %broadcast_in_dim.16), channel_id=1, replica_groups=mesh['z'=12,'x'=4,'pair'=4,'odd'=2,'core'=2] {'x','odd'}, dimensions={0} | all-to-all | bytes 2097152 | tf_op jit(solution)/shard_map/all_to_all | solution.py:140
  67.1 1.9 %collective-permute-start.1 = (f32[8,64,512]{2,1,0:T(8,128)S(1)}, f32[8,64,512]{2,1,0:T(8,128)S(1)}, u32[]{:S(2)}, u32[]{:S(2)}) collective-permute-start(f32[8,64,512]{2,1,0:T(8,128)S(1)} %all_to_all.11.own_ref), channel_id=1, source_target_pairs={{0,1},{1,0},{2,3},{3,2},{4,5},{5,4},{6,7},{7,6},{8,9},{9,8},{10,11... | collective-permute-start | bytes 3145736 | tf_op jit(solution)/shard_map/ppermute | solution.py:141
  69.0 0.0 copy-start
  69.0 1.0 convolution_bitcast_fusion.gram_ref
  70.0 1.6 %collective-permute-done.1.other_ref = f32[8,64,512]{2,1,0:T(8,128)S(1)} collective-permute-done((f32[8,64,512]{2,1,0:T(8,128)S(1)}, f32[8,64,512]{2,1,0:T(8,128)S(1)}, u32[]{:S(2)}, u32[]{:S(2)}) %collective-permute-start.1) | collective-permute-done | bytes 1048608 | tf_op jit(solution)/shard_map/ppermute | solution.py:141
  71.6 0.0 copy-start.1
  71.6 0.0 copy-start.2
  71.6 0.0 copy-done
  71.6 0.6 copy-done.1
  72.3 0.0 copy-done.2
  72.3 2.6 %power.1 = (f32[8,512]{1,0:T(8,128)S(1)}, f32[8,512]{1,0:T(8,128)S(1)}, f32[8,512]{1,0:T(8,128)S(1)}, f32[8,512]{1,0:T(8,128)S(1)}, f32[8,512]{1,0:T(8,128)S(1)}...) custom-call(s32[4]{0:T(128)S(1)} %bitcast.18, ...), custom_call_target="tpu_custom_call" | custom-call | tf_op jit(solution)/shard_map/power/pallas_call | solution.py:149
  74.9 59.8 %all-reduce.2 = (f32[8,512]{1,0:T(8,128)S(1)}, f32[8,512]{1,0:T(8,128)S(1)}, f32[8,512]{1,0:T(8,128)S(1)}, f32[8,512]{1,0:T(8,128)S(1)}, f32[8,512]{1,0:T(8,128)...) all-reduce(f32[8,512]{1,0:T(8,128)S(1)} %get-tuple-element.75, ...), channel_id=1, replica_groups=mesh['z'=12,'x'=4,'pair'=4,'odd'=2,'core'=2] {'z'}, use_global_device_ids=true, to_apply=%region_2.0 | all-reduce | flops 262144 | bytes 2097152 | tf_op jit(solution)/shard_map/psum | solution.py:166
  134.7 1.6 %join.1 = f32[512,512]{1,0:T(8,128)} custom-call(f32[8,512]{1,0:T(8,128)S(1)} %get-tuple-element.141.refs_0_, f32[8,512]{1,0:T(8,128)S(1)} %get-tuple-element.142.refs_1_, f32[8,512]{1,0:T(8,128)S(1)} %get-tuple-element.143.refs_2_, f32[8,512]{1,0:T(8,128)S(1)} %get-tuple-element.144.refs_3_, f32[8,512]{1,0:T(8,128)S(1)} %get-tuple-element.145.refs_4_, ...), custom_call_target="tpu_custom_call" | custom-call | tf_op jit(solution)/shard_map/join/pallas_call | solution.py:167
  (1 shorter events, 0.0 us)
Async XLA Ops:
  3.4 4.6 %collective-permute-start = (f32[512,512]{1,0:T(8,128)S(1)}, f32[512,512]{1,0:T(8,128)S(1)}, u32[]{:S(2)}, u32[]{:S(2)}) collective-permute-start(f32[512,512]{1,0:T(8,128)S(1)} %get-tuple-element.73), channel_id=1, source_target_pairs={{0,1},{1,0},{2,3},{3,2},{4,5},{5,4},{6,7},{7,6},{8,9},{9,8},{10,11... | collective-permute-start | bytes 3145736 | tf_op jit(solution)/shard_map/ppermute | solution.py:134
  67.1 4.5 %collective-permute-start.1 = (f32[8,64,512]{2,1,0:T(8,128)S(1)}, f32[8,64,512]{2,1,0:T(8,128)S(1)}, u32[]{:S(2)}, u32[]{:S(2)}) collective-permute-start(f32[8,64,512]{2,1,0:T(8,128)S(1)} %all_to_all.11.own_ref), channel_id=1, source_target_pairs={{0,1},{1,0},{2,3},{3,2},{4,5},{5,4},{6,7},{7,6},{8,9},{9,8},{10,11... | collective-permute-start | bytes 3145736 | tf_op jit(solution)/shard_map/ppermute | solution.py:141
  69.0 2.6 %copy-start = (bf16[1,1,4,128,128]{4,3,2,1,0:T(8,128)(2,1)S(1)}, bf16[1,1,4,128,128]{4,3,2,1,0:T(8,128)(2,1)}, u32[]{:S(2)}) copy-start(bf16[1,1,4,128,128]{4,3,2,1,0:T(8,128)(2,1)} %param.5) | copy-start | bytes 393220
  71.6 0.7 copy-start.1
  71.6 0.7 copy-start.2

commit v6 on v5

--- a/solution.py
+++ b/solution.py
@@ -47,11 +47,12 @@
 
 
 def power_kernel(
-    rows_ref, cols_ref, live_ref, core_ref, tile_ref, own_ref, other_ref, gram_ref, y_ref, place_ref, *refs
+    table_ref, tile_ref, own_ref, other_ref, gram_ref, y_ref, *refs
 ):
+    slots = tile_ref.shape[0]
     out_refs, (gram_out, y_out, acc_ref, gram_buf, sems) = refs[:-5], refs[-5:]
     share = y_out.shape[0]
-    y_at = pl.ds(pl.multiple_of(place_ref[0] * share, share), share)
+    y_at = pl.ds(pl.multiple_of(table_ref[2 * slots + 2] * share, share), share)
     y_copy = pltpu.make_async_copy(y_ref.at[y_at], y_out, sems.at[0])
     y_copy.start()
     places, sub, width = other_ref.shape
@@ -67,13 +68,13 @@
     gram_copy = pltpu.make_async_copy(gram_buf, gram_out, sems.at[1])
     gram_copy.start()
 
-    own = core_ref[0] == 0
+    own = table_ref[2 * slots + 1] == 0
     acc_ref[...] = jnp.zeros_like(acc_ref)
-    for s in range(tile_ref.shape[0]):
-
-        @pl.when(s < live_ref[0])
+    for s in range(slots):
+
+        @pl.when(s < table_ref[2 * slots])
         def _():
-            row = rows_ref[s]
+            row = table_ref[s]
             at = pl.ds(pl.multiple_of(row % 2 * (2 * part), 2 * part), 2 * part)
             parts = []
             for odd in range(2):
@@ -81,7 +82,7 @@
                 parts.append(jnp.where(own, mine, theirs).reshape(2, part, width))
                 parts.append(jnp.where(own, theirs, mine).reshape(2, part, width))
             y_block = jnp.stack(parts, axis=1).reshape(BLK, width)
-            base = pl.multiple_of(cols_ref[s] * BLK, BLK)
+            base = pl.multiple_of(table_ref[slots + s] * BLK, BLK)
             acc_ref[pl.ds(base, BLK), :] += tile_dot(tile_ref[s], y_block, 0)
 
     at = 0
@@ -143,6 +144,7 @@
         flat = own.reshape(half, width)
         gram = jnp.dot(flat.T, flat, precision=lax.Precision.HIGH, preferred_element_type=f32)
 
+        table = jnp.concatenate(scalars + (place,))
         rows_out = CB_DEV * BLK
         step = rows_out // PIECES
         sizes = [step] * (PIECES - 1) + [step // 2] * 2
@@ -153,7 +155,7 @@
                 jax.ShapeDtypeStruct((width, width), f32),
                 jax.ShapeDtypeStruct((share, width), f32),
             ),
-            in_specs=[SMEM] * 4 + [VMEM] * 5 + [SMEM],
+            in_specs=[SMEM] + [VMEM] * 5,
             out_specs=tuple(VMEM for _ in sizes) + (ANY, ANY),
             scratch_shapes=[
                 pltpu.VMEM((rows_out, width), f32),
@@ -162,7 +164,7 @@
             ],
             compiler_params=PARAMS,
             name="power",
-        )(*scalars, tiles, own, other, gram, chunk, place)
+        )(table, tiles, own, other, gram, chunk)
         pieces = lax.psum(pieces, "z")
         z_power = pl.pallas_call(
             join_kernel,

time: 137 us -> 136 us (level)
  the two profiles are of different devices: /device:TPU:8 before, /device:TPU:16 now
where the time goes in v6:
time: 136 us
  blocking collectives  118 us (87%)
  Pallas kernels  6.4 us (5%)
  starting transfers between devices  3.83 us (3%)
  waiting for transfers between devices  3.45 us (3%)
  between operations  1.37 us (1%)
    psum x1, blocking collectives, local(): pieces = lax.psum(pieces, 'z')  59.8 us
    all_to_all x1, blocking collectives, local(): part = lax.all_to_all(part, ('x', 'odd'), 0, 0, tiled=True).sum(0)  21.1 us
    all_gather x1, blocking collectives, local(): chunk = lax.all_gather(part, 'pair', axis=0, tiled=False).sum(0)  20.2 us
    all_to_all x1, blocking collectives, local(): own = lax.all_to_all(own, ('x', 'odd'), 0, 0, tiled=True)  17.1 us
  transfers between devices with their start and end apart: 2, of which 2 were waited for; matrix products, arithmetic and copies ran while one was open for 1% of the time, Pallas kernels for 0%

profile of v6, /device:TPU:16, one launch (start us, length us, event | category | flops | bytes accessed | tf_op | source)
XLA Modules:
  0.0 135.5 jit_solution(2871330376931133853)
XLA Ops:
  1.3 2.3 %sample.1 = (f32[512,512]{1,0:T(8,128)S(1)}, f32[512,512]{1,0:T(8,128)S(1)}) custom-call(s32[4]{0:T(128)} %bitcast.19, s32[4]{0:T(128)} %bitcast.21, s32[1]{0:T(128)} %bitcast.14.live_ref, s32[1]{0:T(128)} %bitcast.3.core_ref, bf16[4,128,128]{2,1,0:T(8,128)(2,1)} %bitcast.15, f32[512,512]{1,0:T(8,128)} %omega_ref.1), custom_call_target="tpu_custom_call" | custom-call | tf_op jit(solution)/shard_map/sample/pallas_call | solution.py:128
  3.6 1.9 %collective-permute-start = (f32[512,512]{1,0:T(8,128)S(1)}, f32[512,512]{1,0:T(8,128)S(1)}, u32[]{:S(2)}, u32[]{:S(2)}) collective-permute-start(f32[512,512]{1,0:T(8,128)S(1)} %get-tuple-element.73), channel_id=1, source_target_pairs={{0,1},{1,0},{2,3},{3,2},{4,5},{5,4},{6,7},{7,6},{8,9},{9,8},{10,11... | collective-permute-start | bytes 3145736 | tf_op jit(solution)/shard_map/ppermute | solution.py:135
  5.5 2.6 %collective-permute-done = f32[512,512]{1,0:T(8,128)S(1)} collective-permute-done((f32[512,512]{1,0:T(8,128)S(1)}, f32[512,512]{1,0:T(8,128)S(1)}, u32[]{:S(2)}, u32[]{:S(2)}) %collective-permute-start) | collective-permute-done | bytes 1048608 | tf_op jit(solution)/shard_map/ppermute | solution.py:135
  8.1 0.2 add.133
  8.3 21.1 %all_to_all.10 = f32[8,64,512]{2,1,0:T(8,128)S(1)} all-to-all(f32[8,64,512]{2,1,0:T(8,128)S(1)} %bitcast.17), channel_id=1, replica_groups=mesh['z'=12,'x'=4,'pair'=4,'odd'=2,'core'=2] {'x','odd'}, dimensions={0} | all-to-all | bytes 2097152 | tf_op jit(solution)/shard_map/all_to_all | solution.py:138
  29.4 0.1 reduce_sum.18
  29.5 20.2 %all-gather = f32[256,512]{1,0:T(8,128)S(1)} all-gather(f32[64,512]{1,0:T(8,128)S(1)} %reduce_sum.18), channel_id=2, replica_groups=mesh['z'=12,'x'=4,'pair'=4,'odd'=2,'core'=2] {'pair'}, dimensions={0}, use_global_device_ids=true | all-gather | bytes 655360 | tf_op jit(solution)/shard_map/all_gather | solution.py:139
  49.8 0.1 broadcast_in_dim.17
  49.9 17.1 %all_to_all.11.own_ref = f32[8,64,512]{2,1,0:T(8,128)S(1)} all-to-all(f32[8,64,512]{2,1,0:T(8,128)S(1)} %broadcast_in_dim.17), channel_id=1, replica_groups=mesh['z'=12,'x'=4,'pair'=4,'odd'=2,'core'=2] {'x','odd'}, dimensions={0} | all-to-all | bytes 2097152 | tf_op jit(solution)/shard_map/all_to_all | solution.py:141
  67.0 1.9 %collective-permute-start.1 = (f32[8,64,512]{2,1,0:T(8,128)S(1)}, f32[8,64,512]{2,1,0:T(8,128)S(1)}, u32[]{:S(2)}, u32[]{:S(2)}) collective-permute-start(f32[8,64,512]{2,1,0:T(8,128)S(1)} %all_to_all.11.own_ref), channel_id=1, source_target_pairs={{0,1},{1,0},{2,3},{3,2},{4,5},{5,4},{6,7},{7,6},{8,9},{9,8},{10,11... | collective-permute-start | bytes 3145736 | tf_op jit(solution)/shard_map/ppermute | solution.py:142
  68.9 0.0 copy-start.1
  68.9 0.0 copy-start.2
  68.9 0.6 copy-done.1
  69.6 0.0 copy-done.2
  69.6 0.1 concatenate.3.table_ref
  69.7 0.0 copy-start
  69.7 1.0 convolution_bitcast_fusion.gram_ref
  70.7 0.8 collective-permute-done.1.other_ref
  71.5 0.0 copy-done
  71.5 2.6 %power.1 = (f32[8,512]{1,0:T(8,128)S(1)}, f32[8,512]{1,0:T(8,128)S(1)}, f32[8,512]{1,0:T(8,128)S(1)}, f32[8,512]{1,0:T(8,128)S(1)}, f32[8,512]{1,0:T(8,128)S(1)}...) custom-call(s32[11]{0:T(128)S(1)} %concatenate.3.table_ref, ...), custom_call_target="tpu_custom_call" | custom-call | tf_op jit(solution)/shard_map/power/pallas_call | solution.py:151
  74.1 59.8 %all-reduce.2 = (f32[8,512]{1,0:T(8,128)S(1)}, f32[8,512]{1,0:T(8,128)S(1)}, f32[8,512]{1,0:T(8,128)S(1)}, f32[8,512]{1,0:T(8,128)S(1)}, f32[8,512]{1,0:T(8,128)...) all-reduce(f32[8,512]{1,0:T(8,128)S(1)} %get-tuple-element.75, ...), channel_id=1, replica_groups=mesh['z'=12,'x'=4,'pair'=4,'odd'=2,'core'=2] {'z'}, use_global_device_ids=true, to_apply=%region_2.0 | all-reduce | flops 262144 | bytes 2097152 | tf_op jit(solution)/shard_map/psum | solution.py:168
  133.9 1.6 %join.1 = f32[512,512]{1,0:T(8,128)} custom-call(f32[8,512]{1,0:T(8,128)S(1)} %get-tuple-element.141.refs_0_, f32[8,512]{1,0:T(8,128)S(1)} %get-tuple-element.142.refs_1_, f32[8,512]{1,0:T(8,128)S(1)} %get-tuple-element.143.refs_2_, f32[8,512]{1,0:T(8,128)S(1)} %get-tuple-element.144.refs_3_, f32[8,512]{1,0:T(8,128)S(1)} %get-tuple-element.145.refs_4_, ...), custom_call_target="tpu_custom_call" | custom-call | tf_op jit(solution)/shard_map/join/pallas_call | solution.py:169
  (1 shorter events, 0.0 us)
Async XLA Ops:
  3.6 4.6 %collective-permute-start = (f32[512,512]{1,0:T(8,128)S(1)}, f32[512,512]{1,0:T(8,128)S(1)}, u32[]{:S(2)}, u32[]{:S(2)}) collective-permute-start(f32[512,512]{1,0:T(8,128)S(1)} %get-tuple-element.73), channel_id=1, source_target_pairs={{0,1},{1,0},{2,3},{3,2},{4,5},{5,4},{6,7},{7,6},{8,9},{9,8},{10,11... | collective-permute-start | bytes 3145736 | tf_op jit(solution)/shard_map/ppermute | solution.py:135
  67.0 4.5 %collective-permute-start.1 = (f32[8,64,512]{2,1,0:T(8,128)S(1)}, f32[8,64,512]{2,1,0:T(8,128)S(1)}, u32[]{:S(2)}, u32[]{:S(2)}) collective-permute-start(f32[8,64,512]{2,1,0:T(8,128)S(1)} %all_to_all.11.own_ref), channel_id=1, source_target_pairs={{0,1},{1,0},{2,3},{3,2},{4,5},{5,4},{6,7},{7,6},{8,9},{9,8},{10,11... | collective-permute-start | bytes 3145736 | tf_op jit(solution)/shard_map/ppermute | solution.py:142
  68.9 0.7 copy-start.1
  68.9 0.7 copy-start.2
  69.7 1.9 %copy-start = (bf16[1,1,4,128,128]{4,3,2,1,0:T(8,128)(2,1)S(1)}, bf16[1,1,4,128,128]{4,3,2,1,0:T(8,128)(2,1)}, u32[]{:S(2)}) copy-start(bf16[1,1,4,128,128]{4,3,2,1,0:T(8,128)(2,1)} %param.5) | copy-start | bytes 393220

commit v7 on v6

--- a/solution.py
+++ b/solution.py
@@ -40,7 +40,7 @@
             for odd in range(2):
                 first = halves[:, odd, 0].reshape(2 * part, width)
                 second = halves[:, odd, 1].reshape(2 * part, width)
-                at = (row // 2 * 2 + odd) * sub + row % 2 * (2 * part)
+                at = (odd * (RB_DEV // 2) + row // 2) * sub + row % 2 * (2 * part)
                 at = pl.ds(pl.multiple_of(at, 2 * part), 2 * part)
                 keep_ref[at, :] += jnp.where(own, first, second)
                 send_ref[at, :] += jnp.where(own, second, first)
@@ -78,7 +78,7 @@
             at = pl.ds(pl.multiple_of(row % 2 * (2 * part), 2 * part), 2 * part)
             parts = []
             for odd in range(2):
-                mine, theirs = own_ref[row // 2 * 2 + odd, at, :], other_ref[row // 2 * 2 + odd, at, :]
+                mine, theirs = own_ref[odd * (RB_DEV // 2) + row // 2, at, :], other_ref[odd * (RB_DEV // 2) + row // 2, at, :]
                 parts.append(jnp.where(own, mine, theirs).reshape(2, part, width))
                 parts.append(jnp.where(own, theirs, mine).reshape(2, part, width))
             y_block = jnp.stack(parts, axis=1).reshape(BLK, width)
@@ -135,10 +135,10 @@
         part = keep + lax.ppermute(send, "core", swap)
         near, far = nx * 2, ny // 2
         part = part.reshape(near, half // near, width)
-        part = lax.all_to_all(part, ("x", "odd"), 0, 0, tiled=True).sum(0)
+        part = lax.all_to_all(part, ("odd", "x"), 0, 0, tiled=True).sum(0)
         chunk = lax.all_gather(part, "pair", axis=0, tiled=False).sum(0)
         own = jnp.broadcast_to(chunk[None], (near, far * share, width))
-        own = lax.all_to_all(own, ("x", "odd"), 0, 0, tiled=True)
+        own = lax.all_to_all(own, ("odd", "x"), 0, 0, tiled=True)
         other = lax.ppermute(own, "core", swap)
 
         flat = own.reshape(half, width)

time: 136 us -> 135 us (level)
  the two profiles are of different devices: /device:TPU:16 before, /device:TPU:8 now
where the time goes in v7:
time: 135 us
  blocking collectives  118 us (87%)
  Pallas kernels  5.81 us (4%)
  starting transfers between devices  3.83 us (3%)
  waiting for transfers between devices  3.45 us (3%)
  between operations  1.37 us (1%)
    psum x1, blocking collectives, local(): pieces = lax.psum(pieces, 'z')  58.8 us
    all_to_all x1, blocking collectives, local(): part = lax.all_to_all(part, ('odd', 'x'), 0, 0, tiled=True).sum(0)  27.3 us
    all_to_all x1, blocking collectives, local(): own = lax.all_to_all(own, ('odd', 'x'), 0, 0, tiled=True)  16.4 us
    all_gather x1, blocking collectives, local(): chunk = lax.all_gather(part, 'pair', axis=0, tiled=False).sum(0)  16 us
  transfers between devices with their start and end apart: 2, of which 2 were waited for; matrix products, arithmetic and copies ran while one was open for 1% of the time, Pallas kernels for 0%

profile of v7, /device:TPU:8, one launch (start us, length us, event | category | flops | bytes accessed | tf_op | source)
XLA Modules:
  0.0 135.2 jit_solution(9315744092764188216)
XLA Ops:
  1.3 1.7 %sample.1 = (f32[512,512]{1,0:T(8,128)S(1)}, f32[512,512]{1,0:T(8,128)S(1)}) custom-call(s32[4]{0:T(128)} %bitcast.19, s32[4]{0:T(128)} %bitcast.21, s32[1]{0:T(128)} %bitcast.14.live_ref, s32[1]{0:T(128)} %bitcast.3.core_ref, bf16[4,128,128]{2,1,0:T(8,128)(2,1)} %bitcast.15, f32[512,512]{1,0:T(8,128)} %omega_ref.1), custom_call_target="tpu_custom_call" | custom-call | tf_op jit(solution)/shard_map/sample/pallas_call | solution.py:128
  3.0 1.9 %collective-permute-start = (f32[512,512]{1,0:T(8,128)S(1)}, f32[512,512]{1,0:T(8,128)S(1)}, u32[]{:S(2)}, u32[]{:S(2)}) collective-permute-start(f32[512,512]{1,0:T(8,128)S(1)} %get-tuple-element.73), channel_id=1, source_target_pairs={{0,1},{1,0},{2,3},{3,2},{4,5},{5,4},{6,7},{7,6},{8,9},{9,8},{10,11... | collective-permute-start | bytes 3145736 | tf_op jit(solution)/shard_map/ppermute | solution.py:135
  4.9 2.6 %collective-permute-done = f32[512,512]{1,0:T(8,128)S(1)} collective-permute-done((f32[512,512]{1,0:T(8,128)S(1)}, f32[512,512]{1,0:T(8,128)S(1)}, u32[]{:S(2)}, u32[]{:S(2)}) %collective-permute-start) | collective-permute-done | bytes 1048608 | tf_op jit(solution)/shard_map/ppermute | solution.py:135
  7.5 0.2 add.133
  7.7 27.3 %all_to_all.10 = f32[8,64,512]{2,1,0:T(8,128)S(1)} all-to-all(f32[8,64,512]{2,1,0:T(8,128)S(1)} %bitcast.17), channel_id=1, replica_groups=mesh['z'=12,'x'=4,'pair'=4,'odd'=2,'core'=2] {'odd','x'}, dimensions={0} | all-to-all | bytes 2097152 | tf_op jit(solution)/shard_map/all_to_all | solution.py:138
  35.0 0.1 reduce_sum.18
  35.1 16.0 %all-gather = f32[256,512]{1,0:T(8,128)S(1)} all-gather(f32[64,512]{1,0:T(8,128)S(1)} %reduce_sum.18), channel_id=2, replica_groups=mesh['z'=12,'x'=4,'pair'=4,'odd'=2,'core'=2] {'pair'}, dimensions={0}, use_global_device_ids=true | all-gather | bytes 655360 | tf_op jit(solution)/shard_map/all_gather | solution.py:139
  51.1 0.1 broadcast_in_dim.17
  51.3 16.4 %all_to_all.11.own_ref = f32[8,64,512]{2,1,0:T(8,128)S(1)} all-to-all(f32[8,64,512]{2,1,0:T(8,128)S(1)} %broadcast_in_dim.17), channel_id=1, replica_groups=mesh['z'=12,'x'=4,'pair'=4,'odd'=2,'core'=2] {'odd','x'}, dimensions={0} | all-to-all | bytes 2097152 | tf_op jit(solution)/shard_map/all_to_all | solution.py:141
  67.7 1.9 %collective-permute-start.1 = (f32[8,64,512]{2,1,0:T(8,128)S(1)}, f32[8,64,512]{2,1,0:T(8,128)S(1)}, u32[]{:S(2)}, u32[]{:S(2)}) collective-permute-start(f32[8,64,512]{2,1,0:T(8,128)S(1)} %all_to_all.11.own_ref), channel_id=1, source_target_pairs={{0,1},{1,0},{2,3},{3,2},{4,5},{5,4},{6,7},{7,6},{8,9},{9,8},{10,11... | collective-permute-start | bytes 3145736 | tf_op jit(solution)/shard_map/ppermute | solution.py:142
  69.6 0.0 copy-start.1
  69.6 0.0 copy-start.2
  69.6 0.6 copy-done.1
  70.3 0.0 copy-done.2
  70.3 0.1 concatenate.3.table_ref
  70.4 0.0 copy-start
  70.4 1.0 convolution_bitcast_fusion.gram_ref
  71.4 0.8 collective-permute-done.1.other_ref
  72.2 0.0 copy-done
  72.2 2.6 %power.1 = (f32[8,512]{1,0:T(8,128)S(1)}, f32[8,512]{1,0:T(8,128)S(1)}, f32[8,512]{1,0:T(8,128)S(1)}, f32[8,512]{1,0:T(8,128)S(1)}, f32[8,512]{1,0:T(8,128)S(1)}...) custom-call(s32[11]{0:T(128)S(1)} %concatenate.3.table_ref, ...), custom_call_target="tpu_custom_call" | custom-call | tf_op jit(solution)/shard_map/power/pallas_call | solution.py:151
  74.8 58.8 %all-reduce.2 = (f32[8,512]{1,0:T(8,128)S(1)}, f32[8,512]{1,0:T(8,128)S(1)}, f32[8,512]{1,0:T(8,128)S(1)}, f32[8,512]{1,0:T(8,128)S(1)}, f32[8,512]{1,0:T(8,128)...) all-reduce(f32[8,512]{1,0:T(8,128)S(1)} %get-tuple-element.75, ...), channel_id=1, replica_groups=mesh['z'=12,'x'=4,'pair'=4,'odd'=2,'core'=2] {'z'}, use_global_device_ids=true, to_apply=%region_2.0 | all-reduce | flops 262144 | bytes 2097152 | tf_op jit(solution)/shard_map/psum | solution.py:168
  133.6 1.6 %join.1 = f32[512,512]{1,0:T(8,128)} custom-call(f32[8,512]{1,0:T(8,128)S(1)} %get-tuple-element.141.refs_0_, f32[8,512]{1,0:T(8,128)S(1)} %get-tuple-element.142.refs_1_, f32[8,512]{1,0:T(8,128)S(1)} %get-tuple-element.143.refs_2_, f32[8,512]{1,0:T(8,128)S(1)} %get-tuple-element.144.refs_3_, f32[8,512]{1,0:T(8,128)S(1)} %get-tuple-element.145.refs_4_, ...), custom_call_target="tpu_custom_call" | custom-call | tf_op jit(solution)/shard_map/join/pallas_call | solution.py:169
  (1 shorter events, 0.0 us)
Async XLA Ops:
  3.0 4.6 %collective-permute-start = (f32[512,512]{1,0:T(8,128)S(1)}, f32[512,512]{1,0:T(8,128)S(1)}, u32[]{:S(2)}, u32[]{:S(2)}) collective-permute-start(f32[512,512]{1,0:T(8,128)S(1)} %get-tuple-element.73), channel_id=1, source_target_pairs={{0,1},{1,0},{2,3},{3,2},{4,5},{5,4},{6,7},{7,6},{8,9},{9,8},{10,11... | collective-permute-start | bytes 3145736 | tf_op jit(solution)/shard_map/ppermute | solution.py:135
  67.7 4.5 %collective-permute-start.1 = (f32[8,64,512]{2,1,0:T(8,128)S(1)}, f32[8,64,512]{2,1,0:T(8,128)S(1)}, u32[]{:S(2)}, u32[]{:S(2)}) collective-permute-start(f32[8,64,512]{2,1,0:T(8,128)S(1)} %all_to_all.11.own_ref), channel_id=1, source_target_pairs={{0,1},{1,0},{2,3},{3,2},{4,5},{5,4},{6,7},{7,6},{8,9},{9,8},{10,11... | collective-permute-start | bytes 3145736 | tf_op jit(solution)/shard_map/ppermute | solution.py:142
  69.6 0.7 copy-start.1
  69.6 0.7 copy-start.2
  70.4 1.9 %copy-start = (bf16[1,1,4,128,128]{4,3,2,1,0:T(8,128)(2,1)S(1)}, bf16[1,1,4,128,128]{4,3,2,1,0:T(8,128)(2,1)}, u32[]{:S(2)}) copy-start(bf16[1,1,4,128,128]{4,3,2,1,0:T(8,128)(2,1)} %param.5) | copy-start | bytes 393220

commit v8 on v7

--- a/solution.py
+++ b/solution.py
@@ -23,27 +23,25 @@
     )
 
 
-def sample_kernel(rows_ref, cols_ref, live_ref, core_ref, tile_ref, omega_ref, keep_ref, send_ref):
-    own = core_ref[0] == 0
+def sample_kernel(rows_ref, cols_ref, live_ref, core_ref, tile_ref, omega_ref, out_ref):
+    lower = core_ref[0] == 0
     width = omega_ref.shape[1]
-    sub = keep_ref.shape[0] // RB_DEV
+    sub = out_ref.shape[0] // RB_DEV
     part = sub // 4
-    keep_ref[...] = jnp.zeros_like(keep_ref)
-    send_ref[...] = jnp.zeros_like(send_ref)
+    out_ref[...] = jnp.zeros_like(out_ref)
     for s in range(tile_ref.shape[0]):
 
         @pl.when(s < live_ref[0])
         def _():
             base = pl.multiple_of(cols_ref[s] * BLK, BLK)
-            halves = tile_dot(tile_ref[s], omega_ref[pl.ds(base, BLK), :], 1).reshape(2, 2, 2, part, width)
+            tile = tile_ref[s].reshape(4, 2, part, BLK)
+            tile = jnp.where(lower, tile[:, 0], tile[:, 1]).reshape(sub, BLK)
+            prod = tile_dot(tile, omega_ref[pl.ds(base, BLK), :], 1).reshape(2, 2, part, width)
             row = rows_ref[s]
             for odd in range(2):
-                first = halves[:, odd, 0].reshape(2 * part, width)
-                second = halves[:, odd, 1].reshape(2 * part, width)
                 at = (odd * (RB_DEV // 2) + row // 2) * sub + row % 2 * (2 * part)
                 at = pl.ds(pl.multiple_of(at, 2 * part), 2 * part)
-                keep_ref[at, :] += jnp.where(own, first, second)
-                send_ref[at, :] += jnp.where(own, second, first)
+                out_ref[at, :] += prod[:, odd].reshape(2 * part, width)
 
 
 def power_kernel(
@@ -125,13 +123,16 @@
         swap = [(0, 1), (1, 0)]
 
         half_shape = pltpu.VMEM((half, width), f32)
-        keep, send = pl.pallas_call(
+        share_of = pl.pallas_call(
             sample_kernel,
-            out_shape=(half_shape, half_shape),
+            out_shape=half_shape,
             in_specs=[SMEM] * 4 + [VMEM] * 2,
-            out_specs=(VMEM, VMEM),
+            out_specs=VMEM,
+            cost_estimate=pl.CostEstimate(flops=1 << 27, transcendentals=0, bytes_accessed=3 << 20),
             name="sample",
-        )(*scalars, tiles, test_block)
+        )
+        send = share_of(*scalars[:3], 1 - core, tiles, test_block)
+        keep = share_of(*scalars, tiles, test_block)
         part = keep + lax.ppermute(send, "core", swap)
         near, far = nx * 2, ny // 2
         part = part.reshape(near, half // near, width)

time: 135 us -> 136 us (level)
  the two profiles are of different devices: /device:TPU:8 before, /device:TPU:16 now
where the time goes in v8:
time: 136 us
  blocking collectives  119 us (88%)
  Pallas kernels  8 us (6%)
  starting transfers between devices  3.84 us (3%)
  waiting for transfers between devices  1.5 us (1%)
  between operations  1.38 us (1%)
    psum x1, blocking collectives, local(): pieces = lax.psum(pieces, 'z')  60 us
    all_to_all x1, blocking collectives, local(): part = lax.all_to_all(part, ('odd', 'x'), 0, 0, tiled=True).sum(0)  21.2 us
    all_to_all x1, blocking collectives, local(): own = lax.all_to_all(own, ('odd', 'x'), 0, 0, tiled=True)  19.1 us
    all_gather x1, blocking collectives, local(): chunk = lax.all_gather(part, 'pair', axis=0, tiled=False).sum(0)  18.3 us
  transfers between devices with their start and end apart: 2, of which 2 were waited for; matrix products, arithmetic and copies ran while one was open for 1% of the time, Pallas kernels for 1%

profile of v8, /device:TPU:16, one launch (start us, length us, event | category | flops | bytes accessed | tf_op | source)
XLA Modules:
  0.0 135.6 jit_solution(13776746438579991500)
XLA Ops:
  1.3 1.9 %sample.3 = f32[512,512]{1,0:T(8,128)S(1)} custom-call(s32[4]{0:T(128)} %bitcast.21, s32[4]{0:T(128)} %bitcast.24, s32[1]{0:T(128)} %bitcast.15.live_ref, s32[1]{0:T(128)S(6)} %sub.3.core_ref, bf16[4,128,128]{2,1,0:T(8,128)(2,1)} %bitcast.16, f32[512,512]{1,0:T(8,128)} %omega_ref.3), custom_call_target="tpu_custom_call" | custom-call | flops 134217728 | bytes 3145728 | tf_op jit(solution)/shard_map/sample/pallas_call | solution.py:134
  3.2 1.9 %collective-permute-start = (f32[512,512]{1,0:T(8,128)S(1)}, f32[512,512]{1,0:T(8,128)S(1)}, u32[]{:S(2)}, u32[]{:S(2)}) collective-permute-start(f32[512,512]{1,0:T(8,128)S(1)} %sample.3), channel_id=1, source_target_pairs={{0,1},{1,0},{2,3},{3,2},{4,5},{5,4},{6,7},{7,6},{8,9},{9,8},{10,11... | collective-permute-start | bytes 3145736 | tf_op jit(solution)/shard_map/ppermute | solution.py:136
  5.2 1.9 %sample.2 = f32[512,512]{1,0:T(8,128)S(1)} custom-call(s32[4]{0:T(128)} %bitcast.22, s32[4]{0:T(128)} %bitcast.25, s32[1]{0:T(128)} %bitcast.14.live_ref, s32[1]{0:T(128)} %bitcast.3.core_ref, bf16[4,128,128]{2,1,0:T(8,128)(2,1)} %bitcast.17, f32[512,512]{1,0:T(8,128)} %omega_ref.3), custom_call_target="tpu_custom_call" | custom-call | flops 134217728 | bytes 3145728 | tf_op jit(solution)/shard_map/sample/pallas_call | solution.py:135
  7.1 0.7 collective-permute-done
  7.8 0.2 add.133
  8.0 21.2 %all_to_all.10 = f32[8,64,512]{2,1,0:T(8,128)S(1)} all-to-all(f32[8,64,512]{2,1,0:T(8,128)S(1)} %bitcast.19), channel_id=1, replica_groups=mesh['z'=12,'x'=4,'pair'=4,'odd'=2,'core'=2] {'odd','x'}, dimensions={0} | all-to-all | bytes 2097152 | tf_op jit(solution)/shard_map/all_to_all | solution.py:139
  29.2 0.1 reduce_sum.18
  29.3 18.3 %all-gather = f32[256,512]{1,0:T(8,128)S(1)} all-gather(f32[64,512]{1,0:T(8,128)S(1)} %reduce_sum.18), channel_id=2, replica_groups=mesh['z'=12,'x'=4,'pair'=4,'odd'=2,'core'=2] {'pair'}, dimensions={0}, use_global_device_ids=true | all-gather | bytes 655360 | tf_op jit(solution)/shard_map/all_gather | solution.py:140
  47.7 0.1 broadcast_in_dim.17
  47.8 19.1 %all_to_all.11.own_ref = f32[8,64,512]{2,1,0:T(8,128)S(1)} all-to-all(f32[8,64,512]{2,1,0:T(8,128)S(1)} %broadcast_in_dim.17), channel_id=1, replica_groups=mesh['z'=12,'x'=4,'pair'=4,'odd'=2,'core'=2] {'odd','x'}, dimensions={0} | all-to-all | bytes 2097152 | tf_op jit(solution)/shard_map/all_to_all | solution.py:142
  66.9 1.9 %collective-permute-start.1 = (f32[8,64,512]{2,1,0:T(8,128)S(1)}, f32[8,64,512]{2,1,0:T(8,128)S(1)}, u32[]{:S(2)}, u32[]{:S(2)}) collective-permute-start(f32[8,64,512]{2,1,0:T(8,128)S(1)} %all_to_all.11.own_ref), channel_id=1, source_target_pairs={{0,1},{1,0},{2,3},{3,2},{4,5},{5,4},{6,7},{7,6},{8,9},{9,8},{10,11... | collective-permute-start | bytes 3145736 | tf_op jit(solution)/shard_map/ppermute | solution.py:143
  68.8 0.0 copy-start.1
  68.8 0.0 copy-start.2
  68.8 0.6 copy-done.1
  69.4 0.0 copy-done.2
  69.5 0.1 concatenate.3.table_ref
  69.5 0.0 copy-start
  69.5 1.0 convolution_bitcast_fusion.gram_ref
  70.6 0.8 collective-permute-done.1.other_ref
  71.4 0.0 copy-done
  71.4 2.6 %power.1 = (f32[8,512]{1,0:T(8,128)S(1)}, f32[8,512]{1,0:T(8,128)S(1)}, f32[8,512]{1,0:T(8,128)S(1)}, f32[8,512]{1,0:T(8,128)S(1)}, f32[8,512]{1,0:T(8,128)S(1)}...) custom-call(s32[11]{0:T(128)S(1)} %concatenate.3.table_ref, ...), custom_call_target="tpu_custom_call" | custom-call | tf_op jit(solution)/shard_map/power/pallas_call | solution.py:152
  74.0 60.0 %all-reduce.2 = (f32[8,512]{1,0:T(8,128)S(1)}, f32[8,512]{1,0:T(8,128)S(1)}, f32[8,512]{1,0:T(8,128)S(1)}, f32[8,512]{1,0:T(8,128)S(1)}, f32[8,512]{1,0:T(8,128)...) all-reduce(f32[8,512]{1,0:T(8,128)S(1)} %get-tuple-element.71, ...), channel_id=1, replica_groups=mesh['z'=12,'x'=4,'pair'=4,'odd'=2,'core'=2] {'z'}, use_global_device_ids=true, to_apply=%region_2.0 | all-reduce | flops 262144 | bytes 2097152 | tf_op jit(solution)/shard_map/psum | solution.py:169
  134.0 1.6 %join.1 = f32[512,512]{1,0:T(8,128)} custom-call(f32[8,512]{1,0:T(8,128)S(1)} %get-tuple-element.137.refs_0_, f32[8,512]{1,0:T(8,128)S(1)} %get-tuple-element.138.refs_1_, f32[8,512]{1,0:T(8,128)S(1)} %get-tuple-element.139.refs_2_, f32[8,512]{1,0:T(8,128)S(1)} %get-tuple-element.140.refs_3_, f32[8,512]{1,0:T(8,128)S(1)} %get-tuple-element.141.refs_4_, ...), custom_call_target="tpu_custom_call" | custom-call | tf_op jit(solution)/shard_map/join/pallas_call | solution.py:170
  (1 shorter events, 0.0 us)
Async XLA Ops:
  3.2 4.6 %collective-permute-start = (f32[512,512]{1,0:T(8,128)S(1)}, f32[512,512]{1,0:T(8,128)S(1)}, u32[]{:S(2)}, u32[]{:S(2)}) collective-permute-start(f32[512,512]{1,0:T(8,128)S(1)} %sample.3), channel_id=1, source_target_pairs={{0,1},{1,0},{2,3},{3,2},{4,5},{5,4},{6,7},{7,6},{8,9},{9,8},{10,11... | collective-permute-start | bytes 3145736 | tf_op jit(solution)/shard_map/ppermute | solution.py:136
  66.9 4.5 %collective-permute-start.1 = (f32[8,64,512]{2,1,0:T(8,128)S(1)}, f32[8,64,512]{2,1,0:T(8,128)S(1)}, u32[]{:S(2)}, u32[]{:S(2)}) collective-permute-start(f32[8,64,512]{2,1,0:T(8,128)S(1)} %all_to_all.11.own_ref), channel_id=1, source_target_pairs={{0,1},{1,0},{2,3},{3,2},{4,5},{5,4},{6,7},{7,6},{8,9},{9,8},{10,11... | collective-permute-start | bytes 3145736 | tf_op jit(solution)/shard_map/ppermute | solution.py:143
  68.8 0.7 copy-start.1
  68.8 0.7 copy-start.2
  69.5 1.9 %copy-start = (bf16[1,1,4,128,128]{4,3,2,1,0:T(8,128)(2,1)S(1)}, bf16[1,1,4,128,128]{4,3,2,1,0:T(8,128)(2,1)}, u32[]{:S(2)}) copy-start(bf16[1,1,4,128,128]{4,3,2,1,0:T(8,128)(2,1)} %param.5) | copy-start | bytes 393220

commit v9 on v8

--- a/solution.py
+++ b/solution.py
@@ -59,9 +59,12 @@
     hi = v.astype(jnp.bfloat16)
     mid = (v - hi.astype(jnp.float32)).astype(jnp.bfloat16)
     dims = (((0,), (0,)), ((), ()))
-    acc = lax.dot_general(hi, mid, dims, preferred_element_type=jnp.float32)
-    acc += lax.dot_general(mid, hi, dims, preferred_element_type=jnp.float32)
-    acc += lax.dot_general(hi, hi, dims, preferred_element_type=jnp.float32)
+    acc = lax.dot_general(
+        jnp.concatenate([hi, mid, hi], axis=0),
+        jnp.concatenate([mid, hi, hi], axis=0),
+        dims,
+        preferred_element_type=jnp.float32,
+    )
     gram_buf[...] = (gram_ref[...] + acc) * (1.0 / (RB_DEV * BLK))
     gram_copy = pltpu.make_async_copy(gram_buf, gram_out, sems.at[1])
     gram_copy.start()

time: 136 us -> 136 us (level)
  no operation moved by 1% of the time
where the time goes in v9:
time: 136 us; the launch traced here: 137 us
  blocking collectives  120 us (88%)
  Pallas kernels  7.3 us (5%)
  starting transfers between devices  4.19 us (3%)
  waiting for transfers between devices  1.5 us (1%)
  between operations  1.38 us (1%)
    psum x1, blocking collectives, local(): pieces = lax.psum(pieces, 'z')  60.8 us
    all_to_all x1, blocking collectives, local(): part = lax.all_to_all(part, ('odd', 'x'), 0, 0, tiled=True).sum(0)  21.3 us
    all_to_all x1, blocking collectives, local(): own = lax.all_to_all(own, ('odd', 'x'), 0, 0, tiled=True)  19.2 us
    all_gather x1, blocking collectives, local(): chunk = lax.all_gather(part, 'pair', axis=0, tiled=False).sum(0)  18.7 us
  transfers between devices with their start and end apart: 2, of which 2 were waited for; matrix products, arithmetic and copies ran while one was open for 1% of the time, Pallas kernels for 1%

profile of v9, /device:TPU:16, one launch (start us, length us, event | category | flops | bytes accessed | tf_op | source)
XLA Modules:
  0.0 136.6 jit_solution(4001690884270695083)
XLA Ops:
  1.3 1.6 %sample.3 = f32[512,512]{1,0:T(8,128)S(1)} custom-call(s32[4]{0:T(128)} %bitcast.21, s32[4]{0:T(128)} %bitcast.24, s32[1]{0:T(128)} %bitcast.15.live_ref, s32[1]{0:T(128)S(6)} %sub.3.core_ref, bf16[4,128,128]{2,1,0:T(8,128)(2,1)} %bitcast.16, f32[512,512]{1,0:T(8,128)} %omega_ref.3), custom_call_target="tpu_custom_call" | custom-call | flops 134217728 | bytes 3145728 | tf_op jit(solution)/shard_map/sample/pallas_call | solution.py:137
  2.9 2.3 %collective-permute-start = (f32[512,512]{1,0:T(8,128)S(1)}, f32[512,512]{1,0:T(8,128)S(1)}, u32[]{:S(2)}, u32[]{:S(2)}) collective-permute-start(f32[512,512]{1,0:T(8,128)S(1)} %sample.3), channel_id=1, source_target_pairs={{0,1},{1,0},{2,3},{3,2},{4,5},{5,4},{6,7},{7,6},{8,9},{9,8},{10,11... | collective-permute-start | bytes 3145736 | tf_op jit(solution)/shard_map/ppermute | solution.py:139
  5.2 1.6 %sample.2 = f32[512,512]{1,0:T(8,128)S(1)} custom-call(s32[4]{0:T(128)} %bitcast.22, s32[4]{0:T(128)} %bitcast.25, s32[1]{0:T(128)} %bitcast.14.live_ref, s32[1]{0:T(128)} %bitcast.3.core_ref, bf16[4,128,128]{2,1,0:T(8,128)(2,1)} %bitcast.17, f32[512,512]{1,0:T(8,128)} %omega_ref.3), custom_call_target="tpu_custom_call" | custom-call | flops 134217728 | bytes 3145728 | tf_op jit(solution)/shard_map/sample/pallas_call | solution.py:138
  6.7 0.7 collective-permute-done
  7.4 0.2 add.133
  7.6 21.3 %all_to_all.10 = f32[8,64,512]{2,1,0:T(8,128)S(1)} all-to-all(f32[8,64,512]{2,1,0:T(8,128)S(1)} %bitcast.19), channel_id=1, replica_groups=mesh['z'=12,'x'=4,'pair'=4,'odd'=2,'core'=2] {'odd','x'}, dimensions={0} | all-to-all | bytes 2097152 | tf_op jit(solution)/shard_map/all_to_all | solution.py:142
  28.9 0.1 reduce_sum.18
  29.0 18.7 %all-gather = f32[256,512]{1,0:T(8,128)S(1)} all-gather(f32[64,512]{1,0:T(8,128)S(1)} %reduce_sum.18), channel_id=2, replica_groups=mesh['z'=12,'x'=4,'pair'=4,'odd'=2,'core'=2] {'pair'}, dimensions={0}, use_global_device_ids=true | all-gather | bytes 655360 | tf_op jit(solution)/shard_map/all_gather | solution.py:143
  47.7 0.1 broadcast_in_dim.17
  47.8 19.2 %all_to_all.11.own_ref = f32[8,64,512]{2,1,0:T(8,128)S(1)} all-to-all(f32[8,64,512]{2,1,0:T(8,128)S(1)} %broadcast_in_dim.17), channel_id=1, replica_groups=mesh['z'=12,'x'=4,'pair'=4,'odd'=2,'core'=2] {'odd','x'}, dimensions={0} | all-to-all | bytes 2097152 | tf_op jit(solution)/shard_map/all_to_all | solution.py:145
  67.0 1.9 %collective-permute-start.1 = (f32[8,64,512]{2,1,0:T(8,128)S(1)}, f32[8,64,512]{2,1,0:T(8,128)S(1)}, u32[]{:S(2)}, u32[]{:S(2)}) collective-permute-start(f32[8,64,512]{2,1,0:T(8,128)S(1)} %all_to_all.11.own_ref), channel_id=1, source_target_pairs={{0,1},{1,0},{2,3},{3,2},{4,5},{5,4},{6,7},{7,6},{8,9},{9,8},{10,11... | collective-permute-start | bytes 3145736 | tf_op jit(solution)/shard_map/ppermute | solution.py:146
  69.0 0.0 copy-start.1
  69.0 0.0 copy-start.2
  69.0 0.6 copy-done.1
  69.6 0.0 copy-done.2
  69.6 0.1 concatenate.3.table_ref
  69.7 0.0 copy-start
  69.7 1.0 convolution_bitcast_fusion.gram_ref
  70.7 0.8 collective-permute-done.1.other_ref
  71.6 0.0 copy-done
  71.6 2.6 %power.1 = (f32[8,512]{1,0:T(8,128)S(1)}, f32[8,512]{1,0:T(8,128)S(1)}, f32[8,512]{1,0:T(8,128)S(1)}, f32[8,512]{1,0:T(8,128)S(1)}, f32[8,512]{1,0:T(8,128)S(1)}...) custom-call(s32[11]{0:T(128)S(1)} %concatenate.3.table_ref, ...), custom_call_target="tpu_custom_call" | custom-call | tf_op jit(solution)/shard_map/power/pallas_call | solution.py:155
  74.2 60.8 %all-reduce.2 = (f32[8,512]{1,0:T(8,128)S(1)}, f32[8,512]{1,0:T(8,128)S(1)}, f32[8,512]{1,0:T(8,128)S(1)}, f32[8,512]{1,0:T(8,128)S(1)}, f32[8,512]{1,0:T(8,128)...) all-reduce(f32[8,512]{1,0:T(8,128)S(1)} %get-tuple-element.71, ...), channel_id=1, replica_groups=mesh['z'=12,'x'=4,'pair'=4,'odd'=2,'core'=2] {'z'}, use_global_device_ids=true, to_apply=%region_2.0 | all-reduce | flops 262144 | bytes 2097152 | tf_op jit(solution)/shard_map/psum | solution.py:172
  135.0 1.6 %join.1 = f32[512,512]{1,0:T(8,128)} custom-call(f32[8,512]{1,0:T(8,128)S(1)} %get-tuple-element.137.refs_0_, f32[8,512]{1,0:T(8,128)S(1)} %get-tuple-element.138.refs_1_, f32[8,512]{1,0:T(8,128)S(1)} %get-tuple-element.139.refs_2_, f32[8,512]{1,0:T(8,128)S(1)} %get-tuple-element.140.refs_3_, f32[8,512]{1,0:T(8,128)S(1)} %get-tuple-element.141.refs_4_, ...), custom_call_target="tpu_custom_call" | custom-call | tf_op jit(solution)/shard_map/join/pallas_call | solution.py:173
  (1 shorter events, 0.0 us)
Async XLA Ops:
  2.9 4.6 %collective-permute-start = (f32[512,512]{1,0:T(8,128)S(1)}, f32[512,512]{1,0:T(8,128)S(1)}, u32[]{:S(2)}, u32[]{:S(2)}) collective-permute-start(f32[512,512]{1,0:T(8,128)S(1)} %sample.3), channel_id=1, source_target_pairs={{0,1},{1,0},{2,3},{3,2},{4,5},{5,4},{6,7},{7,6},{8,9},{9,8},{10,11... | collective-permute-start | bytes 3145736 | tf_op jit(solution)/shard_map/ppermute | solution.py:139
  67.0 4.5 %collective-permute-start.1 = (f32[8,64,512]{2,1,0:T(8,128)S(1)}, f32[8,64,512]{2,1,0:T(8,128)S(1)}, u32[]{:S(2)}, u32[]{:S(2)}) collective-permute-start(f32[8,64,512]{2,1,0:T(8,128)S(1)} %all_to_all.11.own_ref), channel_id=1, source_target_pairs={{0,1},{1,0},{2,3},{3,2},{4,5},{5,4},{6,7},{7,6},{8,9},{9,8},{10,11... | collective-permute-start | bytes 3145736 | tf_op jit(solution)/shard_map/ppermute | solution.py:146
  69.0 0.7 copy-start.1
  69.0 0.7 copy-start.2
  69.7 1.9 %copy-start = (bf16[1,1,4,128,128]{4,3,2,1,0:T(8,128)(2,1)S(1)}, bf16[1,1,4,128,128]{4,3,2,1,0:T(8,128)(2,1)}, u32[]{:S(2)}) copy-start(bf16[1,1,4,128,128]{4,3,2,1,0:T(8,128)(2,1)} %param.5) | copy-start | bytes 393220
